TPU v7x, 256 devices: a whole 4x4x8 slice. The times are simulated.
256 devices in a mesh: grp: 8 (over z), tp: 32 (over x, y, core).
Axes of the slice: x: 4, y: 4, z: 8, core: 2. Of those that a mesh axis runs over, the one named last changes fastest.
Arguments:
- hidden_in: bfloat16 [1024, 3584], P(('grp', 'tp')), may hold values from -6 to 6
- norm_gains: float32 [4, 3584], replicated, may hold values from 0.25 to 1.75
- w_qkv: bfloat16 [3584, 8192], P(None, 'tp'), may hold values from -0.09375 to 0.09375
- w_out: bfloat16 [4096, 3584], P('tp'), may hold values from -0.09375 to 0.09375
- w_gate_up: bfloat16 [2, 3584, 8192], P(None, None, 'tp'), may hold values from -0.09375 to 0.09375
- w_down: bfloat16 [8192, 3584], P('tp'), may hold values from -0.0625 to 0.0625
- prompt_keys: bfloat16 [32768, 2048], P(('grp', 'tp')), may hold values from -480 to 480, as said below
- prompt_values: bfloat16 [32768, 2048], P(('grp', 'tp')), may hold values from -6 to 6
- tail_keys: bfloat16 [1024, 64, 2048], P(('grp', 'tp')), may hold values from -480 to 480, as said below
- tail_values: bfloat16 [1024, 64, 2048], P(('grp', 'tp')), may hold values from -6 to 6
- prompt_len: int32 [80], replicated, may hold values from 1 to 4087, as said below
- group_home: int32 [80], replicated, may hold values from 0 to 7, as said below
- req_group: int32 [1024], P('grp'), may hold values from 0 to 79, as said below
- tail_len: int32 [1024], P('grp'), may hold values from 1 to 64, 32768 in all
Outputs:
- layer_out: bfloat16 [1024, 3584], P(('grp', 'tp'))
Inputs may be any that keep to these rules, and one draw needn't show every extreme that they name: `group_home`: each grp device is home to exactly 10 groups. `prompt_len`: the prompts of the groups homed on one grp device lie one after another in order of group id from the first of that device's 4096 cache positions; together they hold at most 4096 positions, exactly 4096 on one home in every draw, where one group holds 4087 of them. `req_group`: of the 128 requests held by one grp device, at most 32 belong to groups homed on any one grp device; in every draw one home receives exactly 32 requests from every grp device. `prompt_keys`: cached keys, already rotated. `tail_keys`: cached keys, already rotated.
All inputs are finite; a program needn't handle non-finite values. No bound on the sum of `tail_len` on one device may be relied on, other than what follows from the above.
Results may differ from a plain program's by a relative error of at most 0.015.
Values may be sent and summed in bfloat16 or wider, within the bound.
A program may use at most 128 MiB of HBM per device.

v0:
```python
import math

import jax
import jax.numpy as jnp
from jax import lax
from jax.sharding import PartitionSpec as P

HEADS = 16
KV_HEADS = 8
HEAD_DIM = 256


NORM_EPS = 1e-06
SOFT_CAP = 50.0


def rms_scale(values, gain_row):
    values = values.astype(jnp.float32)
    return (
        values * lax.rsqrt(jnp.mean(values * values, axis=-1, keepdims=True) + NORM_EPS) * gain_row
    )


def rotate(head_rows, position):
    half_width = head_rows.shape[-1] // 2
    freq_index = jnp.arange(half_width).astype(jnp.float32)
    frequency = jnp.exp(freq_index * (-math.log(10000.0) / half_width))
    angles = position.astype(jnp.float32)[:, None] * frequency[None, :]
    cosine = jnp.cos(angles)[:, None, :]
    sine_part = jnp.sin(angles)[:, None, :]
    head_rows = head_rows.astype(jnp.float32)
    first_half = head_rows[..., :half_width]
    second = head_rows[..., half_width:]
    return jnp.concatenate(
        [first_half * cosine - second * sine_part, second * cosine + first_half * sine_part],
        axis=-1,
    )


def capped(scores):
    return SOFT_CAP * jnp.tanh(scores * HEAD_DIM ** (-0.5) / SOFT_CAP)


def lookup(lookup_table, index_list):
    matches = index_list[:, None] == jnp.arange(lookup_table.shape[0], dtype=jnp.int32)[None, :]
    return jnp.sum(jnp.where(matches, lookup_table[None, :], 0), axis=1)


def group_starts(prompt_len, group_home):
    group_ids = jnp.arange(prompt_len.shape[0], dtype=jnp.int32)
    same_home = group_home[:, None] == group_home[None, :]
    earlier = group_ids[None, :] < group_ids[:, None]
    return jnp.sum(jnp.where(same_home & earlier, prompt_len[None, :], 0), axis=1)


def shared_part(queries, key_rows, value_rows, visible):
    scores = capped(
        jnp.einsum("nkjd,pkd->nkjp", queries, key_rows, preferred_element_type=jnp.float32)
    )
    exponent = jnp.where(visible[:, None, None, :], jnp.exp(scores), 0.0)
    numerator = jnp.einsum(
        "nkjp,pkd->nkjd",
        exponent.astype(jnp.bfloat16),
        value_rows,
        preferred_element_type=jnp.float32,
    )
    return (numerator, jnp.sum(exponent, axis=-1))


def own_part(queries, key_rows, value_rows, visible):
    scores = capped(
        jnp.einsum("nkjd,npkd->nkjp", queries, key_rows, preferred_element_type=jnp.float32)
    )
    exponent = jnp.where(visible[:, None, None, :], jnp.exp(scores), 0.0)
    numerator = jnp.einsum(
        "nkjp,npkd->nkjd",
        exponent.astype(jnp.bfloat16),
        value_rows,
        preferred_element_type=jnp.float32,
    )
    return (numerator, jnp.sum(exponent, axis=-1))


def per_device(
    hidden_in,
    norm_gains,
    w_qkv,
    w_out,
    w_gate_up,
    w_down,
    prompt_keys,
    prompt_values,
    tail_keys,
    tail_values,
    prompt_len,
    group_home,
    req_group,
    tail_len,
):
    tp_rank = lax.axis_index("tp")
    q_width = HEADS * HEAD_DIM
    kv_width = KV_HEADS * HEAD_DIM
    row_count = hidden_in.shape[0]
    normed = rms_scale(hidden_in, norm_gains[0]).astype(jnp.bfloat16)
    qkv_share = jnp.dot(
        lax.all_gather(normed, "tp", axis=0, tiled=True), w_qkv, preferred_element_type=jnp.float32
    ).astype(jnp.bfloat16)
    projected_qkv = lax.all_gather(qkv_share, "tp", axis=1, tiled=True)
    requests = projected_qkv.shape[0]
    req_len = lookup(prompt_len, req_group)
    position = req_len + tail_len
    queries = rotate(
        projected_qkv[:, :q_width].reshape(requests, HEADS, HEAD_DIM), position
    ).astype(jnp.bfloat16)
    queries = queries.reshape(requests, KV_HEADS, 2, HEAD_DIM)
    key_new = rotate(
        projected_qkv[:, q_width : q_width + kv_width].reshape(requests, KV_HEADS, HEAD_DIM),
        position,
    ).astype(jnp.bfloat16)
    value_new = projected_qkv[:, q_width + kv_width :].reshape(requests, KV_HEADS, HEAD_DIM)
    starts = group_starts(prompt_len, group_home)
    req_home = lookup(group_home, req_group)
    req_start = lookup(starts, req_group)
    cap_dev = prompt_keys.shape[0]
    row_first = tp_rank * row_count
    own_queries = lax.dynamic_slice_in_dim(queries, row_first, row_count, 0)
    own_tail_len = lax.dynamic_slice_in_dim(tail_len, row_first, row_count, 0)
    tail_dev = tail_keys.shape[1]
    tail_pos = jnp.arange(tail_dev, dtype=jnp.int32)
    own_num, own_den = own_part(
        own_queries,
        tail_keys.reshape(row_count, tail_dev, KV_HEADS, HEAD_DIM),
        tail_values.reshape(row_count, tail_dev, KV_HEADS, HEAD_DIM),
        tail_pos[None, :] < own_tail_len[:, None],
    )
    numerator = lax.dynamic_update_slice_in_dim(
        jnp.zeros((requests, KV_HEADS, 2, HEAD_DIM), jnp.float32), own_num, row_first, 0
    )
    denominator = lax.dynamic_update_slice_in_dim(
        jnp.zeros((requests, KV_HEADS, 2), jnp.float32), own_den, row_first, 0
    )
    key_piece = lax.all_gather(prompt_keys, "grp", axis=0, tiled=True)
    value_piece = lax.all_gather(prompt_values, "grp", axis=0, tiled=True)
    piece_rows = key_piece.shape[0]
    gathered_index = jnp.arange(piece_rows, dtype=jnp.int32)
    home_index = gathered_index // cap_dev
    piece_offsets = tp_rank * cap_dev + gathered_index % cap_dev
    visible = (
        (home_index[None, :] == req_home[:, None])
        & (piece_offsets[None, :] >= req_start[:, None])
        & (piece_offsets[None, :] < (req_start + req_len)[:, None])
    )
    part_num, part_den = shared_part(
        queries,
        key_piece.reshape(piece_rows, KV_HEADS, HEAD_DIM),
        value_piece.reshape(piece_rows, KV_HEADS, HEAD_DIM),
        visible,
    )
    numerator, denominator = (numerator + part_num, denominator + part_den)
    share_width = w_out.shape[0]
    first_col = tp_rank * share_width
    flat_num = numerator.reshape(requests, q_width)
    flat_den = denominator.reshape(requests, HEADS)
    total_num, total_den = lax.psum((flat_num, flat_den), "tp")
    share_num = lax.dynamic_slice_in_dim(total_num, first_col, share_width, 1)
    self_exp = jnp.exp(
        capped(jnp.einsum("nkjd,nkd->nkj", queries, key_new, preferred_element_type=jnp.float32))
    )
    self_num = (
        lax.optimization_barrier(self_exp.astype(jnp.bfloat16)).astype(jnp.float32)[..., None]
        * value_new.astype(jnp.float32)[:, :, None, :]
    )
    self_share = lax.dynamic_slice_in_dim(
        self_num.reshape(requests, q_width), first_col, share_width, 1
    )
    total_den = total_den + self_exp.reshape(requests, HEADS)
    head_of_col = (first_col + jnp.arange(share_width, dtype=jnp.int32)) // HEAD_DIM
    head_pick = (head_of_col[None, :] == jnp.arange(HEADS, dtype=jnp.int32)[:, None]).astype(
        jnp.float32
    )
    den_cols = jnp.dot(total_den, head_pick, precision=lax.Precision.HIGHEST)
    attn_share = ((share_num + self_share) / den_cols).astype(jnp.bfloat16)
    block_rows = attn_share
    attn_proj = lax.psum_scatter(
        jnp.dot(block_rows, w_out, preferred_element_type=jnp.float32),
        "tp",
        scatter_dimension=0,
        tiled=True,
    )
    resid = (hidden_in.astype(jnp.float32) + rms_scale(attn_proj, norm_gains[1])).astype(
        jnp.bfloat16
    )
    ffn_in = rms_scale(resid, norm_gains[2]).astype(jnp.bfloat16)
    gate_up = jnp.einsum(
        "rd,kdf->krf",
        lax.all_gather(ffn_in, "tp", axis=0, tiled=True),
        w_gate_up,
        preferred_element_type=jnp.float32,
    )
    hidden_units = (jax.nn.gelu(gate_up[0], approximate=True) * gate_up[1]).astype(jnp.bfloat16)
    block_rows = hidden_units
    ffn_proj = lax.psum_scatter(
        jnp.dot(block_rows, w_down, preferred_element_type=jnp.float32).astype(jnp.bfloat16),
        "tp",
        scatter_dimension=0,
        tiled=True,
    ).astype(jnp.float32)
    return (resid.astype(jnp.float32) + rms_scale(ffn_proj, norm_gains[3])).astype(jnp.bfloat16)


def solution(mesh):
    in_specs = (
        P(("grp", "tp"), None),
        P(),
        P(None, "tp"),
        P("tp", None),
        P(None, None, "tp"),
        P("tp", None),
        P(("grp", "tp"), None),
        P(("grp", "tp"), None),
        P(("grp", "tp"), None, None),
        P(("grp", "tp"), None, None),
        P(),
        P(),
        P("grp"),
        P("grp"),
    )
    out_specs = P(("grp", "tp"), None)
    return jax.shard_map(
        per_device, mesh=mesh, in_specs=in_specs, out_specs=out_specs, check_vma=False
    )
```

profile of v0, /device:TPU:1, one launch (start us, length us, event | category | flops | bytes accessed | tf_op | source)
XLA Modules:
  0.0 625.6 jit_solution(4266515688802575155)
XLA Ops:
  6.5 1.2 slice_reduce_fusion.1
  7.7 0.9 fusion.35
  8.6 0.8 fusion.47
  9.5 26.6 %all-gather = bf16[32,4,3584]{2,1,0:T(4,128)(2,1)S(1)} all-gather(bf16[1,4,3584]{2,1,0:T(4,128)(2,1)S(1)} %fusion.47), channel_id=1, replica_groups=mesh['grp'=8,'tp'=32] {'tp'}, dimensions={0}, use_global_device_ids=true | all-gather | bytes 946176 | tf_op jit(solution)/shard_map/all_gather | solution.py:106
  36.0 1.1 reshape.279
  37.2 2.9 convolution_convert_fusion.1
  40.1 1.0 copy.77
  41.2 1.0 copy.79
  42.3 0.0 all-reduce.6.cloned.1.call-start
  42.3 0.1 dynamic_slice.12
  42.5 0.2 select_reduce_fusion.2
  42.6 0.1 select_reduce_fusion.3
  42.8 0.1 iota_compare_fusion.4
  42.8 0.3 multiply_cosine_fusion
  43.1 0.9 compare_and_fusion
  44.0 46.5 %all-gather.6.cloned.1.call-done = bf16[128,8192]{1,0:T(8,128)(2,1)} async-done(((bf16[128,256]{1,0:T(8,128)(2,1)}), bf16[128,8192]{1,0:T(8,128)(2,1)}) %all-gather.6.cloned.1.call-update) | async-done | bytes 2097168 | tf_op jit(solution)/shard_map/all_gather | solution.py:108
  90.5 1.4 slice_convert_fusion
  91.9 0.7 copy.101
  92.6 0.3 subtract_convert_fusion
  92.9 0.1 copy.75
  93.1 0.1 copy.76
  93.2 0.9 copy-done.11
  94.1 0.5 fusion.73
  94.6 0.1 copy.88
  94.7 2.4 slice_convert_fusion.2
  97.2 0.3 copy.102
  97.5 0.1 subtract_convert_fusion.1
  97.7 0.1 maximum_bitcast_fusion
  97.8 1.2 pad_maximum_fusion
  98.9 0.3 fusion.10
  99.2 50.9 %all-gather.8.cloned.1.call-done = bf16[1024,2048]{0,1:T(8,128)(2,1)} async-done(((bf16[128,2048]{0,1:T(8,128)(2,1)}), bf16[1024,2048]{0,1:T(8,128)(2,1)}) %all-gather.8.cloned.1.call-update) | async-done | bytes 4194320 | tf_op jit(solution)/shard_map/all_gather | solution.py:142
  150.1 7.7 %bitcast_reduce_fusion = (f32[128,8,2]{0,2,1:T(2,128)S(1)}, f32[8,128,2,1024]{3,1,2,0:T(8,128)}) fusion(pred[128,1024]{1,0:T(8,128)(4,1)} %compare_and_fusion, bf16[1024,8,256,1]{0,2,3,1:T(8,128)(2,1)} %bitcast.96, bf16[128,8,2,128]{3,0,2,1:T(8,128)(2,1)S(1)} %bitcast.87, bf16[128,8,2,128]{3,0,2,1:T(8,128)(2,1)S(1)} %bitcast.84), kind=kOutput, calls=%fused_computation | convolution fusion | flops 1084225536 | bytes 13770752 | tf_op jit(solution)/shard_map/nkjd,pkd->nkjp/dot_general | solution.py:58
  157.8 55.1 %all-gather.10.cloned.1.call-done = bf16[1024,2048]{0,1:T(8,128)(2,1)} async-done(((bf16[128,2048]{0,1:T(8,128)(2,1)}), bf16[1024,2048]{0,1:T(8,128)(2,1)}) %all-gather.10.cloned.1.call-update) | async-done | bytes 4194320 | tf_op jit(solution)/shard_map/all_gather | solution.py:143
  212.9 7.0 %fusion = f32[8,128,2,256]{3,1,2,0:T(8,128)S(1)} fusion(bf16[1024,8,256,1]{0,2,3,1:T(8,128)(2,1)} %bitcast.97, f32[8,128,2,1024]{3,1,2,0:T(8,128)} %get-tuple-element.27, pred[128,1024]{1,0:T(8,128)(4,1)} %compare_and_fusion), kind=kOutput, calls=%fused_computation.4 | convolution fusion | flops 1082130432 | bytes 14811136 | tf_op jit(solution)/shard_map/nkjp,pkd->nkjd/dot_general | solution.py:61
  220.0 1.4 copy.123
  221.3 0.7 fusion.28
  222.0 2.9 copy.85
  224.9 2.9 copy.86
  227.8 0.2 all-reduce.8.cloned.1.call-start
  228.1 3.4 fusion.15
  231.4 1.2 copy.94
  232.7 0.2 copy.87
  232.9 0.3 copy.103
  233.3 2.8 broadcast_multiply_fusion
  236.1 4.0 mul.269
  240.1 0.1 dynamic-slice_add_fusion
  240.2 1.3 add.147
  241.4 67.5 %psum.15 = f32[128,16]{0,1:T(8,128)S(1)} all-reduce(f32[128,16]{0,1:T(8,128)S(1)} %bitcast.94), channel_id=1, replica_groups=mesh['grp'=8,'tp'=32] {'tp'}, use_global_device_ids=true, to_apply=%region_8.9 | all-reduce | flops 2048 | bytes 16384 | tf_op jit(solution)/shard_map/psum | solution.py:164
  309.0 38.9 %all-reduce.6.cloned.1.call-done = f32[128,4096]{1,0:T(8,128)} async-done(((f32[128,4096]{1,0:T(8,128)}), f32[128,4096]{1,0:T(8,128)}) %all-reduce.6.cloned.1.call-update) | async-done | bytes 2097168 | tf_op jit(solution)/shard_map/psum | solution.py:164
  347.9 1.1 fusion.5
  349.1 1.6 fusion.74
  350.7 0.0 all-reduce.10.cloned.1.call-start
  350.8 0.6 dynamic-slice.6
  352.0 115.3 %all-reduce.8.cloned.1.call-done = f32[128,3584]{1,0:T(8,128)} async-done(((f32[128,3584]{1,0:T(8,128)}), f32[128,3584]{1,0:T(8,128)}) %all-reduce.8.cloned.1.call-update) | async-done | bytes 1835024
  467.4 1.0 multiply_reduce_fusion
  468.4 1.1 fusion.39
  469.5 0.1 fusion.46
  469.6 28.2 %all-gather.1 = bf16[32,4,3584]{2,1,0:T(4,128)(2,1)} all-gather(bf16[1,4,3584]{2,1,0:T(4,128)(2,1)S(1)} %fusion.46), channel_id=1, replica_groups=mesh['grp'=8,'tp'=32] {'tp'}, dimensions={0}, use_global_device_ids=true | all-gather | bytes 946176 | tf_op jit(solution)/shard_map/all_gather | solution.py:196
  497.9 1.7 reshape.286
  499.5 2.7 convolution_bitcast_fusion
  502.2 1.4 convolution_convert_fusion
  503.7 112.7 %all-reduce.10.cloned.1.call-done = bf16[128,3584]{1,0:T(8,128)(2,1)} async-done(((bf16[128,3584]{1,0:T(8,128)(2,1)}), bf16[128,3584]{1,0:T(8,128)(2,1)}) %all-reduce.10.cloned.1.call-update) | async-done | bytes 917520
  616.3 1.0 fusion.33
  617.3 1.5 fusion.42
  (45 shorter events, 0.4 us)
Async XLA Ops:
  6.5 495.7 %copy-start = (bf16[256,3584]{1,0:T(8,128)(2,1)S(1)}, bf16[256,3584]{1,0:T(8,128)(2,1)}, u32[]{:S(2)}) copy-start(bf16[256,3584]{1,0:T(8,128)(2,1)} %param.19) | copy-start | bytes 5505028
  6.5 83.9 %all-gather.6.cloned.1.call-start = ((), (), s32[]{:S(2)}) async-start(), calls=%async_computation | async-start | bytes 2162688 | tf_op jit(solution)/shard_map/all_gather | solution.py:108
  36.0 4.1 copy-start.4
  37.2 4.0 copy-start.5
  40.0 2.3 copy-start.10
  40.1 2.4 copy-start.7
  40.1 2.4 copy-start.8
  40.1 2.6 copy-start.9
  40.1 110.0 %all-gather.8.cloned.1.call-start = ((), (), s32[]{:S(2)}) async-start(), calls=%async_computation.1 | async-start | bytes 4718592 | tf_op jit(solution)/shard_map/all_gather | solution.py:142
  41.2 171.8 %all-gather.10.cloned.1.call-start = ((), (), s32[]{:S(2)}) async-start(), calls=%async_computation.2 | async-start | bytes 4718592 | tf_op jit(solution)/shard_map/all_gather | solution.py:143
  42.3 305.7 %all-reduce.6.cloned.1.call-start = ((), (), s32[]{:S(2)}) async-start(), calls=%async_computation.3 | async-start | bytes 4194304 | tf_op jit(solution)/shard_map/psum | solution.py:164
  92.9 1.2 copy-start.11
  97.5 1.4 copy-start.2
  227.8 5.1 copy-start.1
  227.8 239.5 %all-reduce.8.cloned.1.call-start = ((), (), s32[]{:S(2)}) async-start(), calls=%async_computation.4 | async-start | bytes 3670016
  236.1 113.0 %copy-start.3 = (bf16[128,3584]{1,0:T(8,128)(2,1)S(1)}, bf16[128,3584]{1,0:T(8,128)(2,1)}, u32[]{:S(2)}) copy-start(bf16[128,3584]{1,0:T(8,128)(2,1)} %param.17) | copy-start | bytes 2752516
  349.1 1.7 copy-start.12
  349.1 119.3 %copy-start.6 = (bf16[4,3584]{1,0:T(4,128)(2,1)S(1)}, bf16[4,3584]{1,0:T(4,128)(2,1)}, u32[]{:S(2)}) copy-start(bf16[4,3584]{1,0:T(4,128)(2,1)} %param.14) | copy-start | bytes 86020
  350.7 265.6 %all-reduce.10.cloned.1.call-start = ((), (), s32[]{:S(2)}) async-start(), calls=%async_computation.5 | async-start | bytes 1835008
Sparse Core Ops, SparseCore 0:
  40.2 50.2 all-gather.5
  92.2 57.8 all-gather.7
  151.8 61.1 all-gather.9
  228.0 119.9 all-reduce.5
  351.1 116.2 all-reduce.7
  503.8 112.4 all-reduce.9
where the time goes:
time: 626 us
  waiting for transfers between devices  419 us (67%)
  blocking collectives  122 us (19%)
  matrix products  28.5 us (5%)
  local copies, waits for them, and re-layouts  23.3 us (4%)
  other arithmetic  17.2 us (3%)
  between operations  14.4 us (2%)
    unnamed x8, waiting for transfers between devices  228 us
    psum x1, blocking collectives, per_device(): total_num, total_den = lax.psum((flat_num, flat_den), 'tp')  67.5 us
    all_gather x1, waiting for transfers between devices, per_device(): value_piece = lax.all_gather(prompt_values, 'grp', axis=0, tiled=True)  55.1 us
    all_gather x1, waiting for transfers between devices, per_device(): key_piece = lax.all_gather(prompt_keys, 'grp', axis=0, tiled=True)  50.9 us
    all_gather x1, waiting for transfers between devices, per_device(): projected_qkv = lax.all_gather(qkv_share, 'tp', axis=1, tiled=True)  46.5 us
    psum x1, waiting for transfers between devices, per_device(): total_num, total_den = lax.psum((flat_num, flat_den), 'tp')  38.9 us
    all_gather x1, blocking collectives, per_device(): lax.all_gather(ffn_in, 'tp', axis=0, tiled=True)  28.2 us
    all_gather x1, blocking collectives, per_device(): lax.all_gather(normed, 'tp', axis=0, tiled=True)  26.6 us
  transfers between devices with their start and end apart: 6, of which 6 were waited for; matrix products, arithmetic and copies ran while one was open for 5% of the time, Pallas kernels for 0%

commit v1 on v0

v1 whole, which is shorter than its diff:
```python
import functools
import math

import jax
import jax.numpy as jnp
from jax import lax
from jax.experimental import pallas as pl
from jax.experimental.pallas import tpu as pltpu
from jax.sharding import PartitionSpec as P

HEADS = 16
KV_HEADS = 8
HEAD_DIM = 256
SLOTS = 32
NORM_EPS = 1e-06
SOFT_CAP = 50.0
MESH = pl.DeviceIdType.MESH
F32 = jnp.float32
BF16 = jnp.bfloat16


def rms_scale(values, gain_row):
    values = values.astype(F32)
    return (
        values * lax.rsqrt(jnp.mean(values * values, axis=-1, keepdims=True) + NORM_EPS) * gain_row
    )


def capped(scores):
    return SOFT_CAP * jnp.tanh(scores * HEAD_DIM ** (-0.5) / SOFT_CAP)


def lookup(lookup_table, index_list):
    matches = index_list[:, None] == jnp.arange(lookup_table.shape[0], dtype=jnp.int32)[None, :]
    return jnp.sum(jnp.where(matches, lookup_table[None, :], 0), axis=1)


def group_starts(prompt_len, group_home):
    group_ids = jnp.arange(prompt_len.shape[0], dtype=jnp.int32)
    same_home = group_home[:, None] == group_home[None, :]
    earlier = group_ids[None, :] < group_ids[:, None]
    return jnp.sum(jnp.where(same_home & earlier, prompt_len[None, :], 0), axis=1)


def enter(axis, n):
    me = lax.axis_index(axis)
    barrier = pltpu.get_barrier_semaphore()

    def greet(step, carry):
        pl.semaphore_signal(
            barrier, inc=1, device_id={axis: lax.rem(me + step, n)}, device_id_type=MESH
        )
        return carry

    lax.fori_loop(1, n, greet, 0)
    pl.semaphore_wait(barrier, n - 1)


def all_copies(axis, n, source, target, send_sem, recv_sem):
    me = lax.axis_index(axis)

    def outgoing(step):
        peer = lax.rem(me + step, n)
        return pltpu.make_async_remote_copy(
            src_ref=source(peer),
            dst_ref=target.at[me],
            send_sem=send_sem.at[step],
            recv_sem=recv_sem.at[me],
            device_id={axis: peer},
            device_id_type=MESH,
        )

    def incoming(step):
        peer = lax.rem(me + n - step, n)
        return pltpu.make_async_remote_copy(
            src_ref=source(me),
            dst_ref=target.at[peer],
            send_sem=send_sem.at[step],
            recv_sem=recv_sem.at[peer],
            device_id={axis: peer},
            device_id_type=MESH,
        )

    local = pltpu.make_async_copy(source(me), target.at[me], send_sem.at[0])

    def start():
        def one(step, carry):
            outgoing(step).start()
            return carry

        lax.fori_loop(1, n, one, 0)
        local.start()

    def finish():
        def one(step, carry):
            incoming(step).wait_recv()
            outgoing(step).wait_send()
            return carry

        local.wait()
        lax.fori_loop(1, n, one, 0)

    return start, finish


def vmem():
    return pl.BlockSpec(memory_space=pltpu.VMEM)


def params(which):
    return pltpu.CompilerParams(collective_id=which, has_side_effects=True)


def gather(x, axis, n, which):
    def kernel(x_ref, y_ref, send_sem, recv_sem):
        enter(axis, n)
        start, finish = all_copies(axis, n, lambda d: x_ref, y_ref, send_sem, recv_sem)
        start()
        finish()

    return pl.pallas_call(
        kernel,
        out_shape=jax.ShapeDtypeStruct((n, *x.shape), x.dtype),
        in_specs=[vmem()],
        out_specs=vmem(),
        scratch_shapes=[pltpu.SemaphoreType.DMA((n,)), pltpu.SemaphoreType.DMA((n,))],
        compiler_params=params(which),
        name=f"gather{which}",
    )(x)


def swap(x, axis, n, which):
    def kernel(x_ref, y_ref, send_sem, recv_sem):
        enter(axis, n)
        start, finish = all_copies(axis, n, lambda d: x_ref.at[d], y_ref, send_sem, recv_sem)
        start()
        finish()

    return pl.pallas_call(
        kernel,
        out_shape=jax.ShapeDtypeStruct(x.shape, x.dtype),
        in_specs=[vmem()],
        out_specs=vmem(),
        scratch_shapes=[pltpu.SemaphoreType.DMA((n,)), pltpu.SemaphoreType.DMA((n,))],
        compiler_params=params(which),
        name=f"swap{which}",
    )(x)


def place_of(me):
    x, y, core = me // 8, lax.rem(me // 2, 4), lax.rem(me, 2)
    return x, y, core, jnp.where(core == 0, y, 4 + x)


def server_of(head, m):
    return jnp.where(head < 4, (m * 4 + head) * 2, ((head - 4) * 4 + m) * 2 + 1)


def spread_heads(head_rows, n, which):
    rows = head_rows.shape[0]
    own = rows // n

    def kernel(slab_ref, head_ref, own_ref, pair_ref, send_sem, recv_sem, out_sem, in_sem):
        me = lax.axis_index("tp")
        enter("tp", n)
        start, finish = all_copies(
            "tp", n, lambda d: slab_ref.at[d], own_ref, send_sem, recv_sem
        )
        index = lax.rem(me, 2)

        def to_server(m):
            return pltpu.make_async_remote_copy(
                src_ref=head_ref,
                dst_ref=pair_ref.at[index],
                send_sem=out_sem.at[m],
                recv_sem=in_sem.at[index],
                device_id={"tp": server_of(me // 2, m)},
                device_id_type=MESH,
            )

        def local(i):
            return pltpu.make_async_copy(head_ref, pair_ref.at[i], out_sem.at[4])

        for m in range(4):

            @pl.when((me < HEADS) & (server_of(me // 2, m) != me))
            def _():
                to_server(m).start()

        start()
        served = place_of(me)[3]
        for i in range(2):

            @pl.when(2 * served + i == me)
            def _():
                local(i).start()
                local(i).wait()

            @pl.when(2 * served + i != me)
            def _():
                pltpu.make_async_remote_copy(
                    src_ref=head_ref,
                    dst_ref=pair_ref.at[i],
                    send_sem=out_sem.at[5],
                    recv_sem=in_sem.at[i],
                    device_id={"tp": 2 * served + i},
                    device_id_type=MESH,
                ).wait_recv()

        for m in range(4):

            @pl.when((me < HEADS) & (server_of(me // 2, m) != me))
            def _():
                to_server(m).wait_send()

        finish()

    return pl.pallas_call(
        kernel,
        out_shape=[
            jax.ShapeDtypeStruct((n, own, HEAD_DIM), BF16),
            jax.ShapeDtypeStruct((2, rows, HEAD_DIM), BF16),
        ],
        in_specs=[vmem(), vmem()],
        out_specs=[vmem(), vmem()],
        scratch_shapes=[
            pltpu.SemaphoreType.DMA((n,)),
            pltpu.SemaphoreType.DMA((n,)),
            pltpu.SemaphoreType.DMA((6,)),
            pltpu.SemaphoreType.DMA((2,)),
        ],
        compiler_params=params(which),
        name="spread_heads",
    )(head_rows.reshape(n, own, HEAD_DIM), head_rows)


def spread_caches(keys, values, which):
    rows = keys.shape[0]

    def kernel(key_ref, value_ref, keys_ref, values_ref, send_sem, recv_sem, local_sem):
        me = lax.axis_index("tp")
        n = KV_HEADS
        x, y, core, served = place_of(me)
        barrier = pltpu.get_barrier_semaphore()

        def server(head):
            return jnp.where(head < 4, (x * 4 + head) * 2, ((head - 4) * 4 + y) * 2 + 1)

        def source(slot):
            return jnp.where(
                core == 0, (x * 4 + slot // 2) * 2 + lax.rem(slot, 2), (slot // 2 * 4 + y) * 2 + lax.rem(slot, 2)
            )

        for step in range(1, 8):
            pl.semaphore_signal(
                barrier, inc=1, device_id={"tp": x * 8 + lax.rem(me + step, 8)}, device_id_type=MESH
            )
        for step in range(1, 4):
            for other in range(2):
                mate = (lax.rem(x + step, 4) * 4 + y) * 2 + other
                pl.semaphore_signal(barrier, inc=1, device_id={"tp": mate}, device_id_type=MESH)
        pl.semaphore_wait(barrier, 13)

        def copies(head):
            slot = jnp.where(head < 4, y, x) * 2 + core
            columns = pl.ds(pl.multiple_of(head * HEAD_DIM, HEAD_DIM), HEAD_DIM)
            for i, (src, dst) in enumerate(((key_ref, keys_ref), (value_ref, values_ref))):
                yield pltpu.make_async_remote_copy(
                    src_ref=src.at[:, columns],
                    dst_ref=dst.at[slot],
                    send_sem=send_sem.at[i, head],
                    recv_sem=recv_sem.at[i, slot],
                    device_id={"tp": server(head)},
                    device_id_type=MESH,
                )

        def locals_(head):
            slot = jnp.where(core == 0, y, x) * 2 + core
            columns = pl.ds(pl.multiple_of(head * HEAD_DIM, HEAD_DIM), HEAD_DIM)
            for i, (src, dst) in enumerate(((key_ref, keys_ref), (value_ref, values_ref))):
                yield pltpu.make_async_copy(src.at[:, columns], dst.at[slot], local_sem.at[i])

        def arrivals(slot):
            for i, (src, dst) in enumerate(((key_ref, keys_ref), (value_ref, values_ref))):
                yield pltpu.make_async_remote_copy(
                    src_ref=src.at[:, :HEAD_DIM],
                    dst_ref=dst.at[slot],
                    send_sem=send_sem.at[i, 0],
                    recv_sem=recv_sem.at[i, slot],
                    device_id={"tp": source(slot)},
                    device_id_type=MESH,
                )

        for head in range(n):

            @pl.when(server(head) != me)
            def _():
                for copy in copies(head):
                    copy.start()

            @pl.when(server(head) == me)
            def _():
                for copy in locals_(head):
                    copy.start()

        for head in range(n):

            @pl.when(server(head) == me)
            def _():
                for copy in locals_(head):
                    copy.wait()

        for slot in range(n):

            @pl.when(source(slot) != me)
            def _():
                for copy in arrivals(slot):
                    copy.wait_recv()

        for head in range(n):

            @pl.when(server(head) != me)
            def _():
                for copy in copies(head):
                    copy.wait_send()

    block = jax.ShapeDtypeStruct((KV_HEADS, rows, HEAD_DIM), BF16)
    return pl.pallas_call(
        kernel,
        out_shape=[block, block],
        in_specs=[vmem(), vmem()],
        out_specs=[vmem(), vmem()],
        scratch_shapes=[
            pltpu.SemaphoreType.DMA((2, KV_HEADS)),
            pltpu.SemaphoreType.DMA((2, KV_HEADS)),
            pltpu.SemaphoreType.DMA((2,)),
        ],
        compiler_params=params(which),
        name="spread_caches",
    )(keys, values)


def join_parts(slabs, parts, n, which):
    rows = parts.shape[1]

    def kernel(slab_ref, part_ref, own_ref, sums_ref, send_sem, recv_sem, out_sem, in_sem, local_sem):
        me = lax.axis_index("tp")
        enter("tp", n)
        x, y, core, served = place_of(me)
        quarter = jnp.where(core == 0, x, y)
        start, finish = all_copies(
            "tp", n, lambda d: slab_ref.at[d], own_ref, send_sem, recv_sem
        )

        def outgoing(i):
            return pltpu.make_async_remote_copy(
                src_ref=part_ref.at[i],
                dst_ref=sums_ref.at[quarter],
                send_sem=out_sem.at[i],
                recv_sem=in_sem.at[quarter],
                device_id={"tp": 4 * served + i},
                device_id_type=MESH,
            )

        def local(i):
            return pltpu.make_async_copy(part_ref.at[i], sums_ref.at[quarter], local_sem)

        def incoming(m):
            return pltpu.make_async_remote_copy(
                src_ref=part_ref.at[0],
                dst_ref=sums_ref.at[m],
                send_sem=out_sem.at[0],
                recv_sem=in_sem.at[m],
                device_id={"tp": server_of(me // 4, m)},
                device_id_type=MESH,
            )

        for i in range(4):

            @pl.when(4 * served + i != me)
            def _():
                outgoing(i).start()

        start()
        for i in range(4):

            @pl.when(4 * served + i == me)
            def _():
                local(i).start()
                local(i).wait()

        for m in range(4):

            @pl.when(server_of(me // 4, m) != me)
            def _():
                incoming(m).wait_recv()

        for i in range(4):

            @pl.when(4 * served + i != me)
            def _():
                outgoing(i).wait_send()

        finish()

    return pl.pallas_call(
        kernel,
        out_shape=[
            jax.ShapeDtypeStruct(slabs.shape, BF16),
            jax.ShapeDtypeStruct((4, rows, HEAD_DIM), BF16),
        ],
        in_specs=[vmem(), vmem()],
        out_specs=[vmem(), vmem()],
        scratch_shapes=[
            pltpu.SemaphoreType.DMA((n,)),
            pltpu.SemaphoreType.DMA((n,)),
            pltpu.SemaphoreType.DMA((4,)),
            pltpu.SemaphoreType.DMA((4,)),
            pltpu.SemaphoreType.DMA,
        ],
        compiler_params=params(which),
        name="join_parts",
    )(slabs, parts)


def two_words(total):
    high = total.astype(BF16)
    low = (total - lax.optimization_barrier(high).astype(F32)).astype(BF16)
    zeros = jnp.zeros((*total.shape[:-1], 126), BF16)
    return jnp.concatenate([high, low, zeros], axis=-1)


def per_device(
    n,
    planes,
    hidden_in,
    norm_gains,
    w_qkv,
    w_out,
    w_gate_up,
    w_down,
    prompt_keys,
    prompt_values,
    tail_keys,
    tail_values,
    prompt_len,
    group_home,
    req_group,
    tail_len,
):
    me = lax.axis_index("tp")
    x, y, core, _ = place_of(me)
    own, width = hidden_in.shape
    rows = own * n
    normed = rms_scale(hidden_in, norm_gains[0]).astype(BF16)
    key_blocks, value_blocks = spread_caches(prompt_keys, prompt_values, 1)
    normed_all = gather(normed, "tp", n, 0).reshape(rows, width)
    head_rows = jnp.dot(normed_all, w_qkv, preferred_element_type=F32).astype(BF16)

    req_len = lookup(prompt_len, req_group)
    position = req_len + tail_len
    half = HEAD_DIM // 2
    frequency = jnp.exp(jnp.arange(half).astype(F32) * (-math.log(10000.0) / half))
    angles = position.astype(F32)[:, None] * frequency[None, :]
    cosine, sine = jnp.cos(angles), jnp.sin(angles)
    first, second = head_rows[:, :half].astype(F32), head_rows[:, half:].astype(F32)
    rotated = jnp.concatenate(
        [first * cosine - second * sine, second * cosine + first * sine], axis=-1
    ).astype(BF16)
    head_rows = jnp.where(me < HEADS + KV_HEADS, rotated, head_rows)
    own_heads, pair = spread_heads(head_rows, n, 2)

    req_home = lookup(group_home, req_group)
    req_start = lookup(group_starts(prompt_len, group_home), req_group)
    order = jnp.arange(rows, dtype=jnp.int32)
    before = (req_home[None, :] == req_home[:, None]) & (order[None, :] < order[:, None])
    slot = req_home * SLOTS + jnp.sum(before.astype(jnp.int32), axis=1)
    pick = (jnp.arange(planes * SLOTS, dtype=jnp.int32)[:, None] == slot[None, :]).astype(BF16)
    stop = req_start + req_len
    bounds = jnp.stack([req_start // 64, req_start % 64, stop // 64, stop % 64], axis=1).astype(BF16)
    bounds = jnp.pad(bounds, ((0, 0), (0, 124)))
    visit = jnp.concatenate([pair[0], pair[1], bounds], axis=1)
    visit = jnp.dot(pick, visit, preferred_element_type=F32).astype(BF16)
    guests = swap(visit.reshape(planes, SLOTS, 2 * HEAD_DIM + 128), "grp", planes, 3)
    guests = guests.reshape(planes * SLOTS, 2 * HEAD_DIM + 128)

    limits = guests[:, 2 * HEAD_DIM : 2 * HEAD_DIM + 4].astype(F32)
    begin = limits[:, 0:1] * 64 + limits[:, 1:2]
    end = limits[:, 2:3] * 64 + limits[:, 3:4]
    block = jnp.arange(KV_HEADS, dtype=jnp.int32)
    block_device = jnp.where(
        core == 0, (x * 4 + block // 2) * 2 + block % 2, (block // 2 * 4 + y) * 2 + block % 2
    )
    piece = prompt_keys.shape[0]
    spot = (block_device[:, None] * piece + jnp.arange(piece, dtype=jnp.int32)[None, :]).reshape(1, -1)
    spot = spot.astype(F32)
    visible = (spot >= begin) & (spot < end)
    block_keys = key_blocks.reshape(-1, HEAD_DIM)
    block_values = value_blocks.reshape(-1, HEAD_DIM)
    nums, dens = [], []
    for i in range(2):
        query = guests[:, i * HEAD_DIM : (i + 1) * HEAD_DIM]
        scores = capped(
            lax.dot_general(query, block_keys, (((1,), (1,)), ((), ())), preferred_element_type=F32)
        )
        expo = jnp.where(visible, jnp.exp(scores), 0.0)
        nums.append(jnp.dot(expo.astype(BF16), block_values, preferred_element_type=F32).astype(BF16))
        dens.append(jnp.sum(expo, axis=-1, keepdims=True))
    den_words = jnp.concatenate(
        [two_words(dens[0])[:, :2], two_words(dens[1])[:, :2], jnp.zeros((planes * SLOTS, 124), BF16)],
        axis=-1,
    )
    reply = jnp.concatenate([nums[0], nums[1], den_words], axis=1)
    replies = swap(reply.reshape(planes, SLOTS, 2 * HEAD_DIM + 128), "grp", planes, 4)
    replies = replies.reshape(planes * SLOTS, 2 * HEAD_DIM + 128)
    back = lax.dot_general(
        pick, replies, (((0,), (0,)), ((), ())), preferred_element_type=F32
    ).astype(BF16)
    pad = jnp.zeros((rows, 126), BF16)
    parts = jnp.stack(
        [
            jnp.concatenate(
                [
                    back[:, i * 128 : (i + 1) * 128],
                    back[:, 2 * HEAD_DIM + (i // 2) * 2 : 2 * HEAD_DIM + (i // 2) * 2 + 2],
                    pad,
                ],
                axis=1,
            )
            for i in range(4)
        ]
    )

    queries = own_heads[:HEADS].reshape(KV_HEADS, 2, own, HEAD_DIM)
    own_keys, own_values = own_heads[HEADS : HEADS + KV_HEADS], own_heads[HEADS + KV_HEADS :]
    tail = tail_keys.shape[1]
    own_len = lax.dynamic_slice_in_dim(tail_len, me * own, own, 0)
    seen = jnp.arange(tail, dtype=jnp.int32)[None, :] < own_len[:, None]
    tails = tail_keys.reshape(own, tail, KV_HEADS, HEAD_DIM)
    tail_rows = tail_values.reshape(own, tail, KV_HEADS, HEAD_DIM)
    expo = jnp.exp(capped(jnp.einsum("kjnd,npkd->nkjp", queries, tails, preferred_element_type=F32)))
    expo = jnp.where(seen[:, None, None, :], expo, 0.0)
    own_num = jnp.einsum("nkjp,npkd->kjnd", expo.astype(BF16), tail_rows, preferred_element_type=F32)
    own_den = jnp.sum(expo, axis=-1).transpose(1, 2, 0)
    self_exp = jnp.exp(
        capped(jnp.sum(queries.astype(F32) * own_keys[:, None].astype(F32), axis=-1))
    )
    self_weight = lax.optimization_barrier(self_exp.astype(BF16)).astype(F32)
    own_num = own_num + self_weight[..., None] * own_values[:, None].astype(F32)
    own_den = (own_den + self_exp).reshape(HEADS, own, 1)
    own_num = own_num.astype(BF16).reshape(HEADS, own, 2, 128).transpose(0, 2, 1, 3)
    den_lanes = jnp.broadcast_to(two_words(own_den)[:, None], (HEADS, 2, own, 128))
    slabs = jnp.concatenate([own_num, den_lanes], axis=-1).reshape(n, own, 256)

    mine, sums = join_parts(slabs, parts, n, 5)
    total = mine.reshape(rows, 256).astype(F32) + jnp.sum(sums.astype(F32), axis=0)
    attn_share = (total[:, :128] / (total[:, 128:129] + total[:, 129:130])).astype(BF16)
    partial = jnp.dot(attn_share, w_out, preferred_element_type=F32).astype(BF16)
    attn_proj = jnp.sum(swap(partial.reshape(n, own, width), "tp", n, 6).astype(F32), axis=0)
    resid = (hidden_in.astype(F32) + rms_scale(attn_proj, norm_gains[1])).astype(BF16)
    ffn_in = rms_scale(resid, norm_gains[2]).astype(BF16)
    ffn_all = gather(ffn_in, "tp", n, 7).reshape(rows, width)
    gate = jnp.dot(ffn_all, w_gate_up[0], preferred_element_type=F32)
    up = jnp.dot(ffn_all, w_gate_up[1], preferred_element_type=F32)
    hidden_units = (jax.nn.gelu(gate, approximate=True) * up).astype(BF16)
    partial = jnp.dot(hidden_units, w_down, preferred_element_type=F32).astype(BF16)
    ffn_proj = jnp.sum(swap(partial.reshape(n, own, width), "tp", n, 8).astype(F32), axis=0)
    return (resid.astype(F32) + rms_scale(ffn_proj, norm_gains[3])).astype(BF16)


def solution(mesh):
    in_specs = (
        P(("grp", "tp"), None),
        P(),
        P(None, "tp"),
        P("tp", None),
        P(None, None, "tp"),
        P("tp", None),
        P(("grp", "tp"), None),
        P(("grp", "tp"), None),
        P(("grp", "tp"), None, None),
        P(("grp", "tp"), None, None),
        P(),
        P(),
        P("grp"),
        P("grp"),
    )
    return jax.shard_map(
        functools.partial(per_device, mesh.shape["tp"], mesh.shape["grp"]),
        mesh=mesh,
        in_specs=in_specs,
        out_specs=P(("grp", "tp"), None),
        check_vma=False,
    )
```

time: 626 us -> 210 us (0.34)
  waiting for transfers between devices: 419 us -> 0 us
  Pallas kernels: 0 us -> 161 us
  blocking collectives: 122 us -> 0 us
  between operations: 14.4 us -> 0.51 us
  matrix products: 28.5 us -> 18.2 us
  local copies, waits for them, and re-layouts: 23.3 us -> 15.3 us
    unnamed x8 -> x0, waiting for transfers between devices: 228 us -> none
    pallas_call x0 -> x9, Pallas kernels: none -> 161 us  [the longest x4 69.8 us: swap(): pl.pallas_call(kernel, out_shape=jax.ShapeDtypeStruct(x.shape, x.dtype),...]
    all_gather x3 -> x0, waiting for transfers between devices: 153 us -> none  [the longest x1 55.1 us: per_device(): value_piece = lax.all_gather(prompt_values, 'grp', axis=0, tiled=True)]
    psum x1 -> x0, blocking collectives: 67.5 us -> none  [per_device(): total_num, total_den = lax.psum((flat_num, flat_den), 'tp')]
    all_gather x2 -> x0, blocking collectives: 54.8 us -> none  [the longest x1 28.2 us: per_device(): lax.all_gather(ffn_in, 'tp', axis=0, tiled=True)]
    psum x1 -> x0, waiting for transfers between devices: 38.9 us -> none  [per_device(): total_num, total_den = lax.psum((flat_num, flat_den), 'tp')]
    dot_general x10 -> x12, matrix products: 28.5 us -> 18.2 us  [the longest x1 3.66 us: per_device(): jnp.dot(hidden_units, w_down, preferred_element_type=F32).astype(BF16)]
    unnamed x35 -> x21, local copies, waits for them, and re-layouts: 9.03 us -> 0.13 us
  transfers between devices with their start and end apart: 6 -> 0, of which waited for: 6 -> 0; matrix products, arithmetic and copies ran while one was open for 5% -> 0% of each run, Pallas kernels for 0% -> 0%
where the time goes in v1:
time: 210 us; the launch traced here: 207 us
  Pallas kernels  161 us (77%)
  matrix products  18.2 us (9%)
  local copies, waits for them, and re-layouts  15.3 us (7%)
  other arithmetic  12.3 us (6%)
    pallas_call x4, Pallas kernels, swap(): pl.pallas_call(kernel, out_shape=jax.ShapeDtypeStruct(x.shape, x.dtype),...  69.8 us
    pallas_call x2, Pallas kernels, gather(): pl.pallas_call(kernel, out_shape=jax.ShapeDtypeStruct((n, *x.shape), x.dt...  42.3 us
    pallas_call x1, Pallas kernels, join_parts(): pl.pallas_call(kernel, out_shape=[jax.ShapeDtypeStruct(slabs.shape, BF16)...  17.6 us
    pallas_call x1, Pallas kernels, spread_heads(): pl.pallas_call(kernel, out_shape=[jax.ShapeDtypeStruct((n, own, HEAD_DIM)...  16.7 us
    pallas_call x1, Pallas kernels, spread_caches(): pl.pallas_call(kernel, out_shape=[block, block], in_specs=[vmem(), vmem()...  14.2 us

profile of v1, /device:TPU:1, one launch (start us, length us, event | category | flops | bytes accessed | tf_op | source)
XLA Modules:
  0.0 206.9 jit_solution(14176438011403318708)
XLA Ops:
  0.0 1.2 slice_reduce_fusion
  1.2 0.9 fusion.75
  2.1 1.4 fusion.77.x_ref
  3.5 20.7 %gather0.1 = bf16[32,4,3584]{2,1,0:T(4,128)(2,1)} custom-call(bf16[4,3584]{1,0:T(4,128)(2,1)} %fusion.77.x_ref), custom_call_target="tpu_custom_call" | custom-call | tf_op jit(solution)/shard_map/gather0/pallas_call | solution.py:121
  24.3 1.7 reshape.394
  26.0 1.9 convolution_convert_fusion.6
  27.9 0.2 select_reduce_fusion.1
  28.1 0.1 select_reduce_fusion.2
  28.2 0.2 convert_reduce_fusion.3
  28.4 0.3 fusion.67
  28.8 0.6 reshape.395.slab_ref
  29.5 16.7 %spread_heads.1 = (bf16[32,4,256]{2,1,0:T(4,128)(2,1)}, bf16[2,128,256]{2,1,0:T(8,128)(2,1)}) custom-call(bf16[32,4,256]{2,1,0:T(4,128)(2,1)} %reshape.395.slab_ref, bf16[128,256]{1,0:T(8,128)(2,1)} %copy-done.2), custom_call_target="tpu_custom_call" | custom-call | tf_op jit(solution)/shard_map/spread_heads/pallas_call | solution.py:218
  46.2 0.7 slice_convert_fusion
  46.9 0.9 multiply_reduce_fusion
  47.8 0.1 copy.105
  47.9 0.8 slice.92
  48.8 1.7 fusion.99
  50.5 0.1 copy.108
  50.6 0.1 copy.110
  50.7 0.2 copy.112
  50.9 0.2 copy.111
  51.2 0.1 pad.32.clone
  51.2 0.1 maximum_maximum_fusion
  51.4 0.1 copy.106
  51.5 1.5 fusion.23
  53.1 0.6 copy.113
  53.7 14.2 %spread_caches.1 = (bf16[8,128,256]{2,1,0:T(8,128)(2,1)}, bf16[8,128,256]{2,1,0:T(8,128)(2,1)}) custom-call(bf16[128,2048]{1,0:T(8,128)(2,1)} %key_ref.1, bf16[128,2048]{1,0:T(8,128)(2,1)} %value_ref.1), custom_call_target="tpu_custom_call" | custom-call | tf_op jit(solution)/shard_map/spread_caches/pallas_call | solution.py:328
  68.0 0.1 copy.114
  68.2 1.0 convolution_convert_fusion.2
  69.1 17.1 %swap3.1 = bf16[8,32,640]{2,1,0:T(8,128)(2,1)} custom-call(bf16[8,32,640]{2,1,0:T(8,128)(2,1)} %bitcast.120), custom_call_target="tpu_custom_call" | custom-call | tf_op jit(solution)/shard_map/swap3/pallas_call | solution.py:139
  86.2 0.9 slice.120
  87.1 0.1 copy.120
  87.4 1.6 fusion.101
  88.9 0.3 convolution_convert_fusion.5
  89.2 1.6 fusion.102
  90.8 0.3 convolution_convert_fusion.4
  91.1 0.2 convert_element_type.256
  91.4 0.2 concatenate.50
  91.6 0.2 convert_element_type.257
  91.9 0.2 concatenate.51
  92.2 0.9 concatenate.45.x_ref
  93.1 12.1 %swap4.1 = bf16[8,32,640]{2,1,0:T(8,128)(2,1)} custom-call(bf16[8,32,640]{2,1,0:T(8,128)(2,1)} %concatenate.45.x_ref), custom_call_target="tpu_custom_call" | custom-call | tf_op jit(solution)/shard_map/swap4/pallas_call | solution.py:139
  105.2 1.2 convolution_convert_fusion.3
  106.6 0.7 pad_maximum_fusion.part_ref
  107.4 17.6 %join_parts.1 = (bf16[32,4,256]{2,1,0:T(4,128)(2,1)}, bf16[4,128,256]{2,1,0:T(8,128)(2,1)}) custom-call(bf16[32,4,256]{2,1,0:T(4,128)(2,1)} %bitcast.121, bf16[4,128,256]{2,1,0:T(8,128)(2,1)} %pad_maximum_fusion.part_ref), custom_call_target="tpu_custom_call" | custom-call | tf_op jit(solution)/shard_map/join_parts/pallas_call | solution.py:406
  125.0 0.9 reshape.410
  125.8 1.0 convert_reduce_fusion.2
  126.8 0.2 fusion.70
  127.0 1.6 convolution_convert_fusion.1
  128.7 1.1 reshape.407.x_ref
  129.8 21.6 %swap6.1 = bf16[32,4,3584]{2,1,0:T(4,128)(2,1)} custom-call(bf16[32,4,3584]{2,1,0:T(4,128)(2,1)} %reshape.407.x_ref), custom_call_target="tpu_custom_call" | custom-call | tf_op jit(solution)/shard_map/swap6/pallas_call | solution.py:139
  151.4 1.6 convert_reduce_fusion.1
  153.0 0.1 multiply_reduce_fusion.2
  153.1 0.2 fusion.79
  153.4 0.7 fusion.81.x_ref
  154.1 21.6 %gather7.1 = bf16[32,4,3584]{2,1,0:T(4,128)(2,1)} custom-call(bf16[4,3584]{1,0:T(4,128)(2,1)} %fusion.81.x_ref), custom_call_target="tpu_custom_call" | custom-call | tf_op jit(solution)/shard_map/gather7/pallas_call | solution.py:121
  175.6 1.7 reshape.408
  177.3 1.9 fusion.48
  179.3 3.7 %convolution_convert_fusion = bf16[128,3584]{1,0:T(8,128)(2,1)} fusion(bf16[256,3584]{1,0:T(8,128)(2,1)S(1)} %copy-done, f32[128,256]{1,0:T(8,128)S(1)} %fusion.48, bf16[128,3584]{1,0:T(8,128)(2,1)S(1)} %reshape.408, bf16[2,3584,256]{2,1,0:T(8,128)(2,1)} %param.18), kind=kOutput, calls=%fused_computation | convolution fusion | flops 470286336 | bytes 5636096 | tf_op jit(solution)/shard_map/dot_general | solution.py:566
  182.9 2.5 %reshape.409.x_ref = bf16[32,4,3584]{2,1,0:T(4,128)(2,1)} reshape(bf16[128,3584]{1,0:T(8,128)(2,1)} %convolution_convert_fusion) | data formatting | bytes 1835008 | tf_op jit(solution)/shard_map/reshape | solution.py:567
  185.4 19.0 %swap8.1 = bf16[32,4,3584]{2,1,0:T(4,128)(2,1)} custom-call(bf16[32,4,3584]{2,1,0:T(4,128)(2,1)} %reshape.409.x_ref), custom_call_target="tpu_custom_call" | custom-call | tf_op jit(solution)/shard_map/swap8/pallas_call | solution.py:139
  204.4 1.6 convert_reduce_fusion
  206.0 0.1 multiply_reduce_fusion.1
  206.1 0.7 fusion.82
  (58 shorter events, 0.9 us)
Async XLA Ops:
  0.0 179.3 %copy-start = (bf16[256,3584]{1,0:T(8,128)(2,1)S(1)}, bf16[256,3584]{1,0:T(8,128)(2,1)}, u32[]{:S(2)}) copy-start(bf16[256,3584]{1,0:T(8,128)(2,1)} %param.19) | copy-start | bytes 5505028
  25.9 2.0 copy-start.5
  25.9 2.0 copy-start.6
  26.0 2.2 %copy-start.7 = (s32[128]{0:T(128)S(1)}, s32[128]{0:T(128)}, u32[]{:S(2)}) copy-start(s32[128]{0:T(128)} %param.26) | copy-start | bytes 1540
  26.0 2.5 %copy-start.8 = (s32[128]{0:T(128)S(1)}, s32[128]{0:T(128)}, u32[]{:S(2)}) copy-start(s32[128]{0:T(128)} %param.27) | copy-start | bytes 1540
  28.8 0.7 copy-start.2
  50.5 17.6 %copy-start.4 = (bf16[2,128,256]{2,1,0:T(8,128)(2,1)S(1)}, bf16[2,128,256]{2,1,0:T(8,128)(2,1)}, u32[]{:S(2)}) copy-start(bf16[2,128,256]{2,1,0:T(8,128)(2,1)} %get-tuple-element.12) | copy-start | bytes 393220
  68.0 19.4 %copy-start.9 = (bf16[8,128,256]{2,1,0:T(8,128)(2,1)S(1)}, bf16[8,128,256]{2,1,0:T(8,128)(2,1)}, u32[]{:S(2)}) copy-start(bf16[8,128,256]{2,1,0:T(8,128)(2,1)} %get-tuple-element.13) | copy-start | bytes 1572868
  86.2 2.7 %copy-start.1 = (bf16[8,128,256]{2,1,0:T(8,128)(2,1)S(1)}, bf16[8,128,256]{2,1,0:T(8,128)(2,1)}, u32[]{:S(2)}) copy-start(bf16[8,128,256]{2,1,0:T(8,128)(2,1)} %get-tuple-element.14) | copy-start | bytes 1572868
  129.8 23.3 %copy-start.3 = (bf16[4,3584]{1,0:T(4,128)(2,1)S(1)}, bf16[4,3584]{1,0:T(4,128)(2,1)}, u32[]{:S(2)}) copy-start(bf16[4,3584]{1,0:T(4,128)(2,1)} %param.14) | copy-start | bytes 86020

commit v2 on v0

v2 whole, which is shorter than its diff:
```python
import functools
import math

import jax
import jax.numpy as jnp
from jax import lax
from jax.experimental import pallas as pl
from jax.experimental.pallas import tpu as pltpu
from jax.sharding import PartitionSpec as P

HEADS = 16
KV_HEADS = 8
HEAD_DIM = 256
HALF = HEAD_DIM // 2
SLOTS = 32
CHIPS = 16
NORM_EPS = 1e-06
SOFT_CAP = 50.0
WIDE = 2 * HEAD_DIM + 128
MESH = pl.DeviceIdType.MESH
F32 = jnp.float32
BF16 = jnp.bfloat16
CHIP_STEPS = (1, 15, 2, 14, 3, 13, 4, 12, 5, 11, 6, 10, 7, 9, 8)
PLANE_STEPS = (4, 3, 5, 2, 6, 1, 7)


def rms_scale(values, gain_row):
    values = values.astype(F32)
    return (
        values * lax.rsqrt(jnp.mean(values * values, axis=-1, keepdims=True) + NORM_EPS) * gain_row
    )


def capped_exp(scores):
    return jnp.exp(SOFT_CAP * jnp.tanh(scores * (HEAD_DIM ** (-0.5) / SOFT_CAP)))


def lookup(lookup_table, index_list):
    matches = index_list[:, None] == jnp.arange(lookup_table.shape[0], dtype=jnp.int32)[None, :]
    return jnp.sum(jnp.where(matches, lookup_table[None, :], 0), axis=1)


def group_starts(prompt_len, group_home):
    group_ids = jnp.arange(prompt_len.shape[0], dtype=jnp.int32)
    same_home = group_home[:, None] == group_home[None, :]
    earlier = group_ids[None, :] < group_ids[:, None]
    return jnp.sum(jnp.where(same_home & earlier, prompt_len[None, :], 0), axis=1)


def remote(src, dst, send_sem, recv_sem, axis, peer):
    return pltpu.make_async_remote_copy(
        src_ref=src,
        dst_ref=dst,
        send_sem=send_sem,
        recv_sem=recv_sem,
        device_id={axis: peer},
        device_id_type=MESH,
    )


def server_of(head, m):
    return jnp.where(head < 4, (m * 4 + head) * 2, ((head - 4) * 4 + m) * 2 + 1)


def layer_kernel(
    n,
    planes,
    hidden_ref,
    gains_ref,
    cosine_ref,
    sine_ref,
    pick_ref,
    pick_t_ref,
    bounds_ref,
    seen_ref,
    w_qkv_hbm,
    w_out_hbm,
    w_gate_up_hbm,
    w_down_hbm,
    keys_hbm,
    values_hbm,
    tail_keys_hbm,
    tail_values_hbm,
    out_ref,
    w_qkv_ref,
    w_out_ref,
    w_gate_up_ref,
    w_down_ref,
    keys_ref,
    values_ref,
    tail_keys_ref,
    tail_values_ref,
    slab_ref,
    slabs_ref,
    rows_ref,
    key_blocks,
    value_blocks,
    head_ref,
    head_slabs,
    own_heads,
    pair_ref,
    visit_ref,
    guest_ref,
    reply_ref,
    answer_ref,
    query_f,
    key_f,
    value_f,
    own_f,
    own_out,
    mine_ref,
    mine_f,
    parts_ref,
    sums_ref,
    part_ref,
    half_ref,
    chip_ref,
    got_ref,
    load_sem,
    ag_send,
    ag_recv,
    fw_send,
    fw_recv,
    kv_send,
    kv_recv,
    sp_send,
    sp_recv,
    pr_send,
    pr_recv,
    z_send,
    z_recv,
    own_send,
    own_recv,
    jn_send,
    jn_recv,
    hf_send,
    hf_recv,
    rs_send,
    rs_recv,
    self_sem,
):
    me = lax.axis_index("tp")
    plane = lax.axis_index("grp")
    chip, core = me // 2, lax.rem(me, 2)
    x, y = chip // 4, lax.rem(chip, 4)
    partner = chip * 2 + 1 - core
    served = jnp.where(core == 0, y, 4 + x)
    quarter = jnp.where(core == 0, x, y)
    own, width = hidden_ref.shape
    rows = own * n

    loads = [
        pltpu.make_async_copy(src, dst, load_sem.at[i])
        for i, (src, dst) in enumerate(
            (
                (keys_hbm, keys_ref),
                (values_hbm, values_ref),
                (w_qkv_hbm, w_qkv_ref),
                (tail_keys_hbm, tail_keys_ref),
                (tail_values_hbm, tail_values_ref),
                (w_out_hbm, w_out_ref),
                (w_gate_up_hbm, w_gate_up_ref),
                (w_down_hbm, w_down_ref),
            )
        )
    ]
    for load in loads:
        load.start()

    barrier = pltpu.get_barrier_semaphore()
    for step in range(1, n):
        pl.semaphore_signal(
            barrier, inc=1, device_id={"tp": lax.rem(me + step, n)}, device_id_type=MESH
        )
    for step in range(1, planes):
        pl.semaphore_signal(
            barrier, inc=1, device_id={"grp": lax.rem(plane + step, planes)}, device_id_type=MESH
        )
    slab_ref[0] = rms_scale(hidden_ref[...], gains_ref[0:1, :]).astype(BF16)
    pl.semaphore_wait(barrier, n - 1 + planes - 1)

    def at_chip(step):
        return lax.rem(chip + step, CHIPS) * 2 + core

    def from_chip(step):
        return lax.rem(chip + CHIPS - step, CHIPS) * 2 + core

    def gather_copy(turn, step):
        return remote(
            slab_ref.at[turn],
            slabs_ref.at[turn, me],
            ag_send.at[turn, step],
            ag_recv.at[turn, step],
            "tp",
            at_chip(step),
        )

    def forward_copy(turn, step):
        source = from_chip(step)
        return remote(
            slab_ref.at[turn] if step == 0 else slabs_ref.at[turn, source],
            slabs_ref.at[turn, source],
            fw_send.at[turn, step],
            fw_recv.at[turn, step],
            "tp",
            partner,
        )

    def gather_start(turn):
        for step in CHIP_STEPS:
            gather_copy(turn, step).start()
        forward_copy(turn, 0).start()
        slabs_ref[turn, me] = slab_ref[turn]

    def gather_finish(turn):
        for step in CHIP_STEPS:
            gather_copy(turn, step).wait_recv()
            forward_copy(turn, step).start()
        for step in (0, *CHIP_STEPS):
            forward_copy(turn, step).wait_recv()
        for group in range(rows // 16):
            four = [slabs_ref[turn, group * 4 + i].astype(F32) for i in range(4)]
            rows_ref[group * 16 : group * 16 + 16, :] = jnp.concatenate(four, axis=0).astype(BF16)

    def gather_drain(turn):
        for step in CHIP_STEPS:
            gather_copy(turn, step).wait_send()
        for step in (0, *CHIP_STEPS):
            forward_copy(turn, step).wait_send()

    def half_copy(turn, step):
        group = pl.ds(lax.rem(x + step, 4) * 4, 4)
        return remote(
            part_ref.at[turn, 1 - core, group],
            half_ref.at[turn, group],
            hf_send.at[turn, step],
            hf_recv.at[turn, step],
            "tp",
            partner,
        )

    def scatter_copy(turn, step):
        target = lax.rem(chip + step, CHIPS)
        return remote(
            chip_ref.at[turn, target],
            got_ref.at[turn, chip],
            rs_send.at[turn, step],
            rs_recv.at[turn, step],
            "tp",
            target * 2 + core,
        )

    def project(turn, left, weight_ref):
        def chunk(j, carry):
            columns = pl.ds(pl.multiple_of(j * 512, 512), 512)
            block = jnp.dot(left, weight_ref[:, columns], preferred_element_type=F32)
            for d in range(n):
                part_ref[turn, d % 2, d // 2, :, columns] = block[own * d : own * d + own, :].astype(BF16)
            return carry

        lax.fori_loop(0, width // 512, chunk, 0)

    def reduce_scatter(turn):
        for step in (0, 1, 2, 3):
            half_copy(turn, step).start()
        for step in (0, 1, 2, 3):
            half_copy(turn, step).wait_recv()
        for step in (0, *CHIP_STEPS):
            target = lax.rem(chip + step, CHIPS)
            both = part_ref[turn, core, target].astype(F32) + half_ref[turn, target].astype(F32)
            chip_ref[turn, target] = both.astype(BF16)
            if step:
                scatter_copy(turn, step).start()
        total = chip_ref[turn, chip].astype(F32)
        for step in CHIP_STEPS:
            scatter_copy(turn, step).wait_recv()
            total = total + got_ref[turn, lax.rem(chip + CHIPS - step, CHIPS)].astype(F32)
        return total

    def scatter_drain(turn):
        for step in (0, 1, 2, 3):
            half_copy(turn, step).wait_send()
        for step in CHIP_STEPS:
            scatter_copy(turn, step).wait_send()

    gather_start(0)

    def kv_server(head):
        return jnp.where(head < 4, (x * 4 + head) * 2, ((head - 4) * 4 + y) * 2 + 1)

    def kv_source(slot):
        mate = lax.rem(slot, 2)
        return jnp.where(core == 0, (x * 4 + slot // 2) * 2 + mate, (slot // 2 * 4 + y) * 2 + mate)

    pieces = ((keys_ref, key_blocks), (values_ref, value_blocks))
    piece = keys_ref.shape[0]

    def kv_copy(i, head):
        slot = (y if head < 4 else x) * 2 + core
        return remote(
            pieces[i][0].at[:, head * HEAD_DIM : (head + 1) * HEAD_DIM],
            pieces[i][1].at[pl.ds(slot * piece, piece)],
            kv_send.at[i, head],
            kv_recv.at[i, slot],
            "tp",
            kv_server(head),
        )

    def kv_local(i, head):
        slot = (y if head < 4 else x) * 2 + core
        return pltpu.make_async_copy(
            pieces[i][0].at[:, head * HEAD_DIM : (head + 1) * HEAD_DIM],
            pieces[i][1].at[pl.ds(slot * piece, piece)],
            self_sem.at[i],
        )

    def kv_arrival(i, slot):
        return remote(
            pieces[i][0].at[:, :HEAD_DIM],
            pieces[i][1].at[slot * piece : (slot + 1) * piece],
            kv_send.at[i, 0],
            kv_recv.at[i, slot],
            "tp",
            kv_source(slot),
        )

    for i in range(2):
        loads[i].wait()
        for head in range(KV_HEADS):

            @pl.when(kv_server(head) != me)
            def _():
                kv_copy(i, head).start()

            @pl.when(kv_server(head) == me)
            def _():
                kv_local(i, head).start()

    gather_finish(0)
    loads[2].wait()
    head_rows = jnp.dot(rows_ref[...], w_qkv_ref[...], preferred_element_type=F32)
    head_rows = head_rows.astype(BF16).astype(F32)
    first, second = head_rows[:, :HALF], head_rows[:, HALF:]
    cosine, sine = cosine_ref[...], sine_ref[...]
    rotated = jnp.concatenate(
        [first * cosine - second * sine, second * cosine + first * sine], axis=-1
    )
    head_rows = jnp.where(me < HEADS + KV_HEADS, rotated, head_rows)
    head_ref[...] = head_rows.astype(BF16)

    index = lax.rem(me, 2)

    def to_server(m):
        return remote(
            head_ref,
            pair_ref.at[index],
            pr_send.at[m],
            pr_recv.at[index],
            "tp",
            server_of(chip, m),
        )

    for m in range(4):

        @pl.when((me < HEADS) & (server_of(chip, m) != me))
        def _():
            to_server(m).start()

    for d in range(n):
        head_slabs[d] = head_rows[own * d : own * d + own, :].astype(BF16)

    def owner_copy(step):
        peer = lax.rem(me + step, n)
        return remote(
            head_slabs.at[peer], own_heads.at[me], sp_send.at[step], sp_recv.at[step], "tp", peer
        )

    for step in range(1, n):
        owner_copy(step).start()
    own_heads[me] = head_slabs[me]

    for i in range(2):

        @pl.when(2 * served + i == me)
        def _():
            pair_ref[i] = head_ref[...]

        @pl.when(2 * served + i != me)
        def _():
            remote(
                head_ref, pair_ref.at[i], pr_send.at[0], pr_recv.at[i], "tp", 2 * served + i
            ).wait_recv()

    pick = pick_ref[...]
    for i in range(2):
        chosen = jnp.dot(pick, pair_ref[i], preferred_element_type=F32)
        visit_ref[:, i * HEAD_DIM : (i + 1) * HEAD_DIM] = chosen.astype(BF16)
    visit_ref[:, 2 * HEAD_DIM :] = jnp.dot(
        pick, bounds_ref[...], preferred_element_type=F32
    ).astype(BF16)

    def z_copy(turn, step):
        peer = lax.rem(plane + step, planes)
        src, dst = ((visit_ref, guest_ref), (reply_ref, answer_ref))[turn]
        return remote(
            src.at[pl.ds(peer * SLOTS, SLOTS)],
            dst.at[pl.ds(plane * SLOTS, SLOTS)],
            z_send.at[turn, step],
            z_recv.at[turn, step],
            "grp",
            peer,
        )

    here = pl.ds(pl.multiple_of(plane * SLOTS, SLOTS), SLOTS)
    for step in PLANE_STEPS:
        z_copy(0, step).start()
    guest_ref[here, :] = visit_ref[here, :]

    for step in range(1, n):
        owner_copy(step).wait_recv()
    for head in range(HEADS):
        block = own_heads[head].astype(F32)
        for r in range(own):
            query_f[r, head : head + 1, :] = block[r : r + 1, :]
    for head in range(KV_HEADS):
        new_key = own_heads[HEADS + head].astype(F32)
        new_value = own_heads[HEADS + KV_HEADS + head].astype(F32)
        for r in range(own):
            for i in range(2):
                spot = 2 * head + i
                key_f[r, spot : spot + 1, :] = new_key[r : r + 1, :]
                value_f[r, spot : spot + 1, :] = new_value[r : r + 1, :]
    loads[3].wait()
    loads[4].wait()
    head_of_row = lax.broadcasted_iota(jnp.int32, (HEADS, HEAD_DIM), 0) // 2
    for r in range(own):
        query = query_f[r]
        spread = jnp.concatenate(
            [jnp.where(head_of_row == k, query, 0.0) for k in range(KV_HEADS)], axis=1
        ).astype(BF16)
        scores = lax.dot_general(
            spread, tail_keys_ref[r], (((1,), (1,)), ((), ())), preferred_element_type=F32
        )
        expo = capped_exp(scores) * seen_ref[r : r + 1, :]
        every = jnp.dot(expo.astype(BF16), tail_values_ref[r], preferred_element_type=F32)
        num = jnp.zeros((HEADS, HEAD_DIM), F32)
        for k in range(KV_HEADS):
            num = jnp.where(head_of_row == k, every[:, k * HEAD_DIM : (k + 1) * HEAD_DIM], num)
        self_exp = capped_exp(jnp.sum(query * key_f[r], axis=-1, keepdims=True))
        num = num + self_exp.astype(BF16).astype(F32) * value_f[r]
        den = jnp.sum(expo, axis=-1, keepdims=True) + self_exp
        den = jnp.broadcast_to(den, (HEADS, 128))
        for head in range(HEADS):
            own_f[head, r : r + 1, :HEAD_DIM] = num[head : head + 1, :]
            own_f[head, r : r + 1, HEAD_DIM:] = den[head : head + 1, :]
    lane = lax.broadcasted_iota(jnp.int32, (own, 128), 1)
    for head in range(HEADS):
        den = own_f[head, :, HEAD_DIM:]
        high = den.astype(BF16).astype(F32)
        words = jnp.where(lane == 0, high, jnp.where(lane == 1, den - high, 0.0)).astype(BF16)
        for i in range(2):
            own_out[2 * head + i, :, :128] = own_f[head, :, i * 128 : (i + 1) * 128].astype(BF16)
            own_out[2 * head + i, :, 128:] = words

    def column_copy(step):
        peer = lax.rem(me + step, n)
        return remote(
            own_out.at[peer], mine_ref.at[me], own_send.at[step], own_recv.at[step], "tp", peer
        )

    for step in range(1, n):
        column_copy(step).start()
    mine_ref[me] = own_out[me]

    for i in range(2):
        for head in range(KV_HEADS):

            @pl.when(kv_server(head) == me)
            def _():
                kv_local(i, head).wait()

        for slot in range(KV_HEADS):

            @pl.when(kv_source(slot) != me)
            def _():
                kv_arrival(i, slot).wait_recv()

    for step in PLANE_STEPS:
        z_copy(0, step).wait_recv()
    at = lax.broadcasted_iota(jnp.int32, (1, KV_HEADS * piece), 1)
    block = at // piece
    pair_of, mate = block // 2, lax.rem(block, 2)
    device = jnp.where(core == 0, (x * 4 + pair_of) * 2 + mate, (pair_of * 4 + y) * 2 + mate)
    spot = (device * piece + lax.rem(at, piece)).astype(F32)
    many = planes * SLOTS // 2
    lanes = lax.broadcasted_iota(jnp.int32, (many, 128), 1)
    for j in range(2):
        part = slice(j * many, (j + 1) * many)
        limits = guest_ref[part, 2 * HEAD_DIM :].astype(F32)
        begin = limits[:, 0:1] * 64 + limits[:, 1:2]
        end = limits[:, 2:3] * 64 + limits[:, 3:4]
        visible = (spot >= begin) & (spot < end)
        words = jnp.zeros((many, 128), F32)
        for i in range(2):
            span = slice(i * HEAD_DIM, (i + 1) * HEAD_DIM)
            scores = lax.dot_general(
                guest_ref[part, span],
                key_blocks[...],
                (((1,), (1,)), ((), ())),
                preferred_element_type=F32,
            )
            expo = jnp.where(visible, capped_exp(scores), 0.0)
            num = jnp.dot(expo.astype(BF16), value_blocks[...], preferred_element_type=F32)
            reply_ref[part, span] = num.astype(BF16)
            den = jnp.sum(expo, axis=-1, keepdims=True)
            high = den.astype(BF16).astype(F32)
            words = jnp.where(lanes == 2 * i, high, words)
            words = jnp.where(lanes == 2 * i + 1, den - high, words)
        reply_ref[part, 2 * HEAD_DIM :] = words.astype(BF16)
    for step in PLANE_STEPS:
        z_copy(1, step).start()
    answer_ref[here, :] = reply_ref[here, :]
    for step in PLANE_STEPS:
        z_copy(1, step).wait_recv()

    back = jnp.dot(pick_t_ref[...], answer_ref[...], preferred_element_type=F32).astype(BF16)
    for i in range(4):
        parts_ref[i, :, :128] = back[:, i * 128 : (i + 1) * 128]
        parts_ref[i, :, 128:] = back[:, 2 * HEAD_DIM :]

    def join_copy(i):
        return remote(
            parts_ref.at[i],
            sums_ref.at[quarter],
            jn_send.at[i],
            jn_recv.at[quarter],
            "tp",
            4 * served + i,
        )

    for i in range(4):

        @pl.when(4 * served + i != me)
        def _():
            join_copy(i).start()

        @pl.when(4 * served + i == me)
        def _():
            sums_ref[quarter] = parts_ref[i]

    for step in range(1, n):
        column_copy(step).wait_recv()
    for p in range(n // 2):
        mine_f[2 * own * p : 2 * own * (p + 1), :] = jnp.concatenate(
            [mine_ref[2 * p].astype(F32), mine_ref[2 * p + 1].astype(F32)], axis=0
        )
    for m in range(4):

        @pl.when(server_of(me // 4, m) != me)
        def _():
            remote(
                parts_ref.at[0],
                sums_ref.at[m],
                jn_send.at[0],
                jn_recv.at[m],
                "tp",
                server_of(me // 4, m),
            ).wait_recv()

    num = mine_f[:, :128]
    den = mine_f[:, 128:129] + mine_f[:, 129:130]
    lower = lax.rem(me, 4) < 2
    for m in range(4):
        num = num + sums_ref[m, :, :128].astype(F32)
        words = sums_ref[m, :, 128:].astype(F32)
        den = den + jnp.where(lower, words[:, 0:1] + words[:, 1:2], words[:, 2:3] + words[:, 3:4])
    attn = (num / den).astype(BF16)

    loads[5].wait()
    project(0, attn, w_out_ref)
    attn_proj = reduce_scatter(0)
    resid = hidden_ref[...].astype(F32) + rms_scale(attn_proj, gains_ref[1:2, :])
    resid = resid.astype(BF16).astype(F32)
    slab_ref[1] = rms_scale(resid, gains_ref[2:3, :]).astype(BF16)
    gather_start(1)
    gather_finish(1)
    loads[6].wait()
    loads[7].wait()
    gate = jnp.dot(rows_ref[...], w_gate_up_ref[0], preferred_element_type=F32)
    up = jnp.dot(rows_ref[...], w_gate_up_ref[1], preferred_element_type=F32)
    bent = jnp.tanh(math.sqrt(2.0 / math.pi) * (gate + 0.044715 * gate * gate * gate))
    hidden_units = (0.5 * gate * (1.0 + bent) * up).astype(BF16)
    project(1, hidden_units, w_down_ref)
    ffn_proj = reduce_scatter(1)
    out_ref[...] = (resid + rms_scale(ffn_proj, gains_ref[3:4, :])).astype(BF16)

    for turn in range(2):
        gather_drain(turn)
        scatter_drain(turn)
        for step in PLANE_STEPS:
            z_copy(turn, step).wait_send()
    for i in range(2):
        for head in range(KV_HEADS):

            @pl.when(kv_server(head) != me)
            def _():
                kv_copy(i, head).wait_send()

    for m in range(4):

        @pl.when((me < HEADS) & (server_of(chip, m) != me))
        def _():
            to_server(m).wait_send()

        @pl.when(4 * served + m != me)
        def _():
            join_copy(m).wait_send()

    for step in range(1, n):
        owner_copy(step).wait_send()
        column_copy(step).wait_send()


def layer(n, planes, small, large):
    own, width = small[0].shape
    rows = own * n
    piece = large[4].shape[0]
    dma = pltpu.SemaphoreType.DMA

    def bf(*shape):
        return pltpu.VMEM(shape, BF16)

    def f32(*shape):
        return pltpu.VMEM(shape, F32)

    slots = planes * SLOTS
    scratch = [
        *(bf(*a.shape) for a in large),
        bf(2, own, width),
        bf(2, n, own, width),
        bf(rows, width),
        bf(KV_HEADS * piece, HEAD_DIM),
        bf(KV_HEADS * piece, HEAD_DIM),
        bf(rows, HEAD_DIM),
        bf(n, own, HEAD_DIM),
        bf(n, own, HEAD_DIM),
        bf(2, rows, HEAD_DIM),
        bf(slots, WIDE),
        bf(slots, WIDE),
        bf(slots, WIDE),
        bf(slots, WIDE),
        f32(own, HEADS, HEAD_DIM),
        f32(own, HEADS, HEAD_DIM),
        f32(own, HEADS, HEAD_DIM),
        f32(HEADS, own, HEAD_DIM + 128),
        bf(n, own, HEAD_DIM),
        bf(n, own, HEAD_DIM),
        f32(rows, HEAD_DIM),
        bf(4, rows, HEAD_DIM),
        bf(4, rows, HEAD_DIM),
        bf(2, 2, CHIPS, own, width),
        bf(2, CHIPS, own, width),
        bf(2, CHIPS, own, width),
        bf(2, CHIPS, own, width),
        dma((8,)),
        dma((2, CHIPS)),
        dma((2, CHIPS)),
        dma((2, CHIPS)),
        dma((2, CHIPS)),
        dma((2, KV_HEADS)),
        dma((2, KV_HEADS)),
        dma((n,)),
        dma((n,)),
        dma((4,)),
        dma((2,)),
        dma((2, planes)),
        dma((2, planes)),
        dma((n,)),
        dma((n,)),
        dma((4,)),
        dma((4,)),
        dma((2, 4)),
        dma((2, 4)),
        dma((2, CHIPS)),
        dma((2, CHIPS)),
        dma((2,)),
    ]
    return pl.pallas_call(
        functools.partial(layer_kernel, n, planes),
        out_shape=jax.ShapeDtypeStruct((own, width), BF16),
        in_specs=[pl.BlockSpec(memory_space=pltpu.VMEM)] * len(small)
        + [pl.BlockSpec(memory_space=pl.ANY)] * len(large),
        out_specs=pl.BlockSpec(memory_space=pltpu.VMEM),
        scratch_shapes=scratch,
        compiler_params=pltpu.CompilerParams(
            collective_id=0, has_side_effects=True, vmem_limit_bytes=60 * 1024 * 1024
        ),
        name="layer",
    )(*small, *large)


def per_device(
    n,
    planes,
    hidden_in,
    norm_gains,
    w_qkv,
    w_out,
    w_gate_up,
    w_down,
    prompt_keys,
    prompt_values,
    tail_keys,
    tail_values,
    prompt_len,
    group_home,
    req_group,
    tail_len,
):
    me = lax.axis_index("tp")
    own = hidden_in.shape[0]
    rows = own * n
    req_len = lookup(prompt_len, req_group)
    position = req_len + tail_len
    frequency = jnp.exp(jnp.arange(HALF).astype(F32) * (-math.log(10000.0) / HALF))
    angles = position.astype(F32)[:, None] * frequency[None, :]
    req_home = lookup(group_home, req_group)
    req_start = lookup(group_starts(prompt_len, group_home), req_group)
    order = jnp.arange(rows, dtype=jnp.int32)
    before = (req_home[None, :] == req_home[:, None]) & (order[None, :] < order[:, None])
    slot = req_home * SLOTS + jnp.sum(before.astype(jnp.int32), axis=1)
    slot_ids = jnp.arange(planes * SLOTS, dtype=jnp.int32)
    pick = (slot_ids[:, None] == slot[None, :]).astype(BF16)
    pick_t = (slot_ids[None, :] == slot[:, None]).astype(BF16)
    stop = req_start + req_len
    bounds = jnp.stack([req_start // 64, req_start % 64, stop // 64, stop % 64], axis=1).astype(BF16)
    bounds = jnp.pad(bounds, ((0, 0), (0, 124)))
    own_len = lax.dynamic_slice_in_dim(tail_len, me * own, own, 0)
    tail = tail_keys.shape[1]
    seen = (jnp.arange(tail, dtype=jnp.int32)[None, :] < own_len[:, None]).astype(F32)
    return layer(
        n,
        planes,
        (hidden_in, norm_gains, jnp.cos(angles), jnp.sin(angles), pick, pick_t, bounds, seen),
        (w_qkv, w_out, w_gate_up, w_down, prompt_keys, prompt_values, tail_keys, tail_values),
    )


def solution(mesh):
    in_specs = (
        P(("grp", "tp"), None),
        P(),
        P(None, "tp"),
        P("tp", None),
        P(None, None, "tp"),
        P("tp", None),
        P(("grp", "tp"), None),
        P(("grp", "tp"), None),
        P(("grp", "tp"), None, None),
        P(("grp", "tp"), None, None),
        P(),
        P(),
        P("grp"),
        P("grp"),
    )
    return jax.shard_map(
        functools.partial(per_device, mesh.shape["tp"], mesh.shape["grp"]),
        mesh=mesh,
        in_specs=in_specs,
        out_specs=P(("grp", "tp"), None),
        check_vma=False,
    )
```

time: 626 us -> 105 us (0.17)
  waiting for transfers between devices: 419 us -> 0 us
  blocking collectives: 122 us -> 0 us
  Pallas kernels: 0 us -> 95.8 us
  matrix products: 28.5 us -> 0 us
  local copies, waits for them, and re-layouts: 23.3 us -> 2.84 us
  between operations: 14.4 us -> 0.04 us
  other arithmetic: 17.2 us -> 5.53 us
    unnamed x8 -> x0, waiting for transfers between devices: 228 us -> none
    all_gather x3 -> x0, waiting for transfers between devices: 153 us -> none  [the longest x1 55.1 us: per_device(): value_piece = lax.all_gather(prompt_values, 'grp', axis=0, tiled=True)]
    pallas_call x0 -> x1, Pallas kernels: none -> 95.8 us  [layer(): pl.pallas_call(functools.partial(layer_kernel, n, planes), out_shape=jax....]
    psum x1 -> x0, blocking collectives: 67.5 us -> none  [per_device(): total_num, total_den = lax.psum((flat_num, flat_den), 'tp')]
    all_gather x2 -> x0, blocking collectives: 54.8 us -> none  [the longest x1 28.2 us: per_device(): lax.all_gather(ffn_in, 'tp', axis=0, tiled=True)]
    psum x1 -> x0, waiting for transfers between devices: 38.9 us -> none  [per_device(): total_num, total_den = lax.psum((flat_num, flat_den), 'tp')]
    dot_general x10 -> x0, matrix products: 28.5 us -> none  [the longest x1 7.73 us: shared_part(): jnp.einsum('nkjd,pkd->nkjp', queries, key_rows, preferred_element_type=jn...]
    unnamed x35 -> x1, local copies, waits for them, and re-layouts: 9.03 us -> 1.37 us
  transfers between devices with their start and end apart: 6 -> 0, of which waited for: 6 -> 0; matrix products, arithmetic and copies ran while one was open for 5% -> 0% of each run, Pallas kernels for 0% -> 0%
where the time goes in v2:
time: 105 us; the launch traced here: 104 us
  Pallas kernels  95.8 us (91%)
  other arithmetic  5.53 us (5%)
  local copies, waits for them, and re-layouts  2.84 us (3%)
    pallas_call x1, Pallas kernels, layer(): pl.pallas_call(functools.partial(layer_kernel, n, planes), out_shape=jax....  95.8 us

profile of v2, /device:TPU:1, one launch (start us, length us, event | category | flops | bytes accessed | tf_op | source)
XLA Modules:
  0.0 104.2 jit_solution(4627766313064620349)
XLA Ops:
  0.0 0.7 dynamic_slice.3
  0.7 0.9 select_reduce_fusion.1
  1.7 0.8 select_reduce_fusion
  2.5 0.2 convert_reduce_fusion
  2.6 0.7 multiply_add_fusion
  3.3 0.6 fusion.4.seen_ref
  4.0 0.1 copy.22
  4.1 0.6 pad.4.bounds_ref
  4.7 0.7 fusion.1.pick_t_ref
  5.4 0.6 fusion.pick_ref
  6.1 0.9 multiply_sine_fusion
  7.0 95.8 %layer.1 = bf16[4,3584]{1,0:T(4,128)(2,1)} custom-call(bf16[4,3584]{1,0:T(4,128)(2,1)} %hidden_ref.1, f32[4,3584]{1,0:T(4,128)} %gains_ref.1, f32[128,128]{1,0:T(8,128)} %get-tuple-element.11.cosine_ref, f32[128,128]{1,0:T(8,128)} %get-tuple-element.10.sine_ref, bf16[256,128]{1,0:T(8,128)(2,1)} %fusion.pick_ref, bf16[128,256]{1,0:T(8,128)(2,1)} %fusion.1.pick_t_ref, ...), custom_call_target="tpu_custom_call" | custom-call | tf_op jit(solution)/shard_map/layer/pallas_call | solution.py:688
  102.8 1.4 %copy.24 = bf16[4,3584]{1,0:T(4,128)(2,1)} copy(bf16[4,3584]{1,0:T(4,128)(2,1)} %layer.1) | data formatting | bytes 57344
  (3 shorter events, 0.0 us)

commit v3 on v2

--- a/solution.py
+++ b/solution.py
@@ -35,18 +35,6 @@
     return jnp.exp(SOFT_CAP * jnp.tanh(scores * (HEAD_DIM ** (-0.5) / SOFT_CAP)))
 
 
-def lookup(lookup_table, index_list):
-    matches = index_list[:, None] == jnp.arange(lookup_table.shape[0], dtype=jnp.int32)[None, :]
-    return jnp.sum(jnp.where(matches, lookup_table[None, :], 0), axis=1)
-
-
-def group_starts(prompt_len, group_home):
-    group_ids = jnp.arange(prompt_len.shape[0], dtype=jnp.int32)
-    same_home = group_home[:, None] == group_home[None, :]
-    earlier = group_ids[None, :] < group_ids[:, None]
-    return jnp.sum(jnp.where(same_home & earlier, prompt_len[None, :], 0), axis=1)
-
-
 def remote(src, dst, send_sem, recv_sem, axis, peer):
     return pltpu.make_async_remote_copy(
         src_ref=src,
@@ -67,12 +55,10 @@
     planes,
     hidden_ref,
     gains_ref,
-    cosine_ref,
-    sine_ref,
-    pick_ref,
-    pick_t_ref,
-    bounds_ref,
-    seen_ref,
+    prompt_len_ref,
+    group_home_ref,
+    req_group_ref,
+    tail_len_ref,
     w_qkv_hbm,
     w_out_hbm,
     w_gate_up_hbm,
@@ -116,6 +102,11 @@
     half_ref,
     chip_ref,
     got_ref,
+    word_ref,
+    words_ref,
+    bound_ref,
+    limit_ref,
+    table_ref,
     load_sem,
     ag_send,
     ag_recv,
@@ -138,6 +129,10 @@
     rs_send,
     rs_recv,
     self_sem,
+    wd_send,
+    wd_recv,
+    lm_send,
+    lm_recv,
 ):
     me = lax.axis_index("tp")
     plane = lax.axis_index("grp")
@@ -285,6 +280,74 @@
 
     gather_start(0)
 
+    table_ref[...] = jnp.full((8, 128), -1.0, F32)
+    groups = prompt_len_ref.shape[1]
+    table_ref[0:1, :groups] = prompt_len_ref[...].astype(F32)
+    table_ref[1:2, :groups] = group_home_ref[...].astype(F32)
+    table_ref[2:3, :] = req_group_ref[...].astype(F32)
+    table_ref[3:4, :] = tail_len_ref[...].astype(F32)
+    len_row, home_row = table_ref[0:1, :], table_ref[1:2, :]
+    tail_row = table_ref[3:4, :]
+    down = lax.broadcasted_iota(jnp.int32, (128, 128), 0)
+    along = lax.broadcasted_iota(jnp.int32, (128, 128), 1)
+    unit = (down == along).astype(BF16)
+    line = lax.broadcasted_iota(jnp.int32, (8, 128), 0)
+
+    def stacked(*lines):
+        total = jnp.zeros((8, 128), F32)
+        for i, value in enumerate(lines):
+            total = jnp.where(line == i, value, total)
+        return total.astype(BF16)
+
+    def split(value):
+        high = jnp.floor(value * (1 / 64))
+        return high, value - 64 * high
+
+    def turned(left, right):
+        return lax.dot_general(left, right, (((1,), (1,)), ((), ())), preferred_element_type=F32)
+
+    columns = turned(unit, stacked(*split(len_row), home_row, table_ref[2:3, :], tail_row))
+    len_column = columns[:, 0:1] * 64 + columns[:, 1:2]
+    earlier = (columns[:, 2:3] == home_row) & (down < along)
+    start_row = jnp.sum(jnp.where(earlier, len_column, 0.0), axis=0, keepdims=True)
+    of_group = stacked(*split(len_row), home_row, *split(start_row))
+    chosen = (columns[:, 3:4] == along.astype(F32)).astype(BF16)
+    req = turned(chosen, of_group)
+    req_row = turned(of_group, chosen)
+    req_len = req[:, 0:1] * 64 + req[:, 1:2]
+    req_stop = req[:, 3:4] * 64 + req[:, 4:5] + req_len
+    same = req[:, 2:3] == req_row[2:3, :]
+    rank = jnp.sum(jnp.where(same & (along < down), 1.0, 0.0), axis=1, keepdims=True)
+    rank_row = jnp.sum(jnp.where(same & (down < along), 1.0, 0.0), axis=0, keepdims=True)
+    slots = planes * SLOTS
+    slot_down = lax.broadcasted_iota(jnp.int32, (slots, rows), 0).astype(F32)
+    slot_along = lax.broadcasted_iota(jnp.int32, (rows, slots), 1).astype(F32)
+    pick = (slot_down == req_row[2:3, :] * SLOTS + rank_row).astype(BF16)
+    pick_t = (slot_along == req[:, 2:3] * SLOTS + rank).astype(BF16)
+    bounds = jnp.zeros((rows, 128), F32)
+    for i, value in enumerate((req[:, 3:4], req[:, 4:5], *split(req_stop))):
+        bounds = jnp.where(along == i, value, bounds)
+    bound_ref[...] = jnp.dot(pick, bounds.astype(BF16), preferred_element_type=F32).astype(BF16)
+
+    def limit_copy(step):
+        peer = lax.rem(plane + step, planes)
+        return remote(
+            bound_ref.at[pl.ds(peer * SLOTS, SLOTS)],
+            limit_ref.at[pl.ds(plane * SLOTS, SLOTS)],
+            lm_send.at[step],
+            lm_recv.at[step],
+            "grp",
+            peer,
+        )
+
+    here = pl.ds(pl.multiple_of(plane * SLOTS, SLOTS), SLOTS)
+    for step in PLANE_STEPS:
+        limit_copy(step).start()
+    limit_ref[here, :] = bound_ref[here, :]
+    frequency = jnp.exp(along[0:1, :].astype(F32) * (-math.log(10000.0) / HALF))
+    angles = (req_len + columns[:, 4:5]) * frequency
+    cosine, sine = jnp.cos(angles), jnp.sin(angles)
+
     def kv_server(head):
         return jnp.where(head < 4, (x * 4 + head) * 2, ((head - 4) * 4 + y) * 2 + 1)
 
@@ -324,24 +387,11 @@
             kv_source(slot),
         )
 
-    for i in range(2):
-        loads[i].wait()
-        for head in range(KV_HEADS):
-
-            @pl.when(kv_server(head) != me)
-            def _():
-                kv_copy(i, head).start()
-
-            @pl.when(kv_server(head) == me)
-            def _():
-                kv_local(i, head).start()
-
     gather_finish(0)
     loads[2].wait()
     head_rows = jnp.dot(rows_ref[...], w_qkv_ref[...], preferred_element_type=F32)
     head_rows = head_rows.astype(BF16).astype(F32)
     first, second = head_rows[:, :HALF], head_rows[:, HALF:]
-    cosine, sine = cosine_ref[...], sine_ref[...]
     rotated = jnp.concatenate(
         [first * cosine - second * sine, second * cosine + first * sine], axis=-1
     )
@@ -391,13 +441,9 @@
                 head_ref, pair_ref.at[i], pr_send.at[0], pr_recv.at[i], "tp", 2 * served + i
             ).wait_recv()
 
-    pick = pick_ref[...]
     for i in range(2):
         chosen = jnp.dot(pick, pair_ref[i], preferred_element_type=F32)
         visit_ref[:, i * HEAD_DIM : (i + 1) * HEAD_DIM] = chosen.astype(BF16)
-    visit_ref[:, 2 * HEAD_DIM :] = jnp.dot(
-        pick, bounds_ref[...], preferred_element_type=F32
-    ).astype(BF16)
 
     def z_copy(turn, step):
         peer = lax.rem(plane + step, planes)
@@ -411,10 +457,21 @@
             peer,
         )
 
-    here = pl.ds(pl.multiple_of(plane * SLOTS, SLOTS), SLOTS)
     for step in PLANE_STEPS:
         z_copy(0, step).start()
     guest_ref[here, :] = visit_ref[here, :]
+
+    for i in range(2):
+        loads[i].wait()
+        for head in range(KV_HEADS):
+
+            @pl.when(kv_server(head) != me)
+            def _():
+                kv_copy(i, head).start()
+
+            @pl.when(kv_server(head) == me)
+            def _():
+                kv_local(i, head).start()
 
     for step in range(1, n):
         owner_copy(step).wait_recv()
@@ -432,6 +489,7 @@
                 value_f[r, spot : spot + 1, :] = new_value[r : r + 1, :]
     loads[3].wait()
     loads[4].wait()
+    tail_at = lax.broadcasted_iota(jnp.int32, (HEADS, tail_keys_ref.shape[1]), 1).astype(F32)
     head_of_row = lax.broadcasted_iota(jnp.int32, (HEADS, HEAD_DIM), 0) // 2
     for r in range(own):
         query = query_f[r]
@@ -441,7 +499,10 @@
         scores = lax.dot_general(
             spread, tail_keys_ref[r], (((1,), (1,)), ((), ())), preferred_element_type=F32
         )
-        expo = capped_exp(scores) * seen_ref[r : r + 1, :]
+        length = jnp.sum(
+            jnp.where(along[0:1, :] == me * own + r, tail_row, 0.0), axis=-1, keepdims=True
+        )
+        expo = jnp.where(tail_at < length, capped_exp(scores), 0.0)
         every = jnp.dot(expo.astype(BF16), tail_values_ref[r], preferred_element_type=F32)
         num = jnp.zeros((HEADS, HEAD_DIM), F32)
         for k in range(KV_HEADS):
@@ -487,6 +548,8 @@
 
     for step in PLANE_STEPS:
         z_copy(0, step).wait_recv()
+    for step in PLANE_STEPS:
+        limit_copy(step).wait_recv()
     at = lax.broadcasted_iota(jnp.int32, (1, KV_HEADS * piece), 1)
     block = at // piece
     pair_of, mate = block // 2, lax.rem(block, 2)
@@ -496,7 +559,7 @@
     lanes = lax.broadcasted_iota(jnp.int32, (many, 128), 1)
     for j in range(2):
         part = slice(j * many, (j + 1) * many)
-        limits = guest_ref[part, 2 * HEAD_DIM :].astype(F32)
+        limits = limit_ref[part, :].astype(F32)
         begin = limits[:, 0:1] * 64 + limits[:, 1:2]
         end = limits[:, 2:3] * 64 + limits[:, 3:4]
         visible = (spot >= begin) & (spot < end)
@@ -523,10 +586,10 @@
     for step in PLANE_STEPS:
         z_copy(1, step).wait_recv()
 
-    back = jnp.dot(pick_t_ref[...], answer_ref[...], preferred_element_type=F32).astype(BF16)
+    back = jnp.dot(pick_t, answer_ref[...], preferred_element_type=F32).astype(BF16)
     for i in range(4):
-        parts_ref[i, :, :128] = back[:, i * 128 : (i + 1) * 128]
-        parts_ref[i, :, 128:] = back[:, 2 * HEAD_DIM :]
+        parts_ref[i] = back[:, i * 128 : (i + 1) * 128]
+    word_ref[...] = turned(unit[:16, :], back[:, 2 * HEAD_DIM :]).astype(BF16)
 
     def join_copy(i):
         return remote(
@@ -538,15 +601,27 @@
             4 * served + i,
         )
 
+    def word_copy(i):
+        return remote(
+            word_ref,
+            words_ref.at[quarter],
+            wd_send.at[i],
+            wd_recv.at[quarter],
+            "tp",
+            4 * served + i,
+        )
+
     for i in range(4):
 
         @pl.when(4 * served + i != me)
         def _():
             join_copy(i).start()
+            word_copy(i).start()
 
         @pl.when(4 * served + i == me)
         def _():
             sums_ref[quarter] = parts_ref[i]
+            words_ref[quarter] = word_ref[...]
 
     for step in range(1, n):
         column_copy(step).wait_recv()
@@ -566,14 +641,23 @@
                 "tp",
                 server_of(me // 4, m),
             ).wait_recv()
+            remote(
+                word_ref,
+                words_ref.at[m],
+                wd_send.at[0],
+                wd_recv.at[m],
+                "tp",
+                server_of(me // 4, m),
+            ).wait_recv()
 
     num = mine_f[:, :128]
     den = mine_f[:, 128:129] + mine_f[:, 129:130]
-    lower = lax.rem(me, 4) < 2
     for m in range(4):
-        num = num + sums_ref[m, :, :128].astype(F32)
-        words = sums_ref[m, :, 128:].astype(F32)
-        den = den + jnp.where(lower, words[:, 0:1] + words[:, 1:2], words[:, 2:3] + words[:, 3:4])
+        num = num + sums_ref[m].astype(F32)
+        words = turned(unit, words_ref[m])
+        which = lax.broadcasted_iota(jnp.int32, words.shape, 1)
+        words = jnp.where(which // 2 == lax.rem(me, 4) // 2, words, 0.0)
+        den = den + jnp.sum(words, axis=-1, keepdims=True)
     attn = (num / den).astype(BF16)
 
     loads[5].wait()
@@ -592,13 +676,15 @@
     hidden_units = (0.5 * gate * (1.0 + bent) * up).astype(BF16)
     project(1, hidden_units, w_down_ref)
     ffn_proj = reduce_scatter(1)
-    out_ref[...] = (resid + rms_scale(ffn_proj, gains_ref[3:4, :])).astype(BF16)
+    out_ref[...] = resid + rms_scale(ffn_proj, gains_ref[3:4, :])
 
     for turn in range(2):
         gather_drain(turn)
         scatter_drain(turn)
         for step in PLANE_STEPS:
             z_copy(turn, step).wait_send()
+    for step in PLANE_STEPS:
+        limit_copy(step).wait_send()
     for i in range(2):
         for head in range(KV_HEADS):
 
@@ -615,6 +701,7 @@
         @pl.when(4 * served + m != me)
         def _():
             join_copy(m).wait_send()
+            word_copy(m).wait_send()
 
     for step in range(1, n):
         owner_copy(step).wait_send()
@@ -645,8 +732,8 @@
         bf(n, own, HEAD_DIM),
         bf(n, own, HEAD_DIM),
         bf(2, rows, HEAD_DIM),
-        bf(slots, WIDE),
-        bf(slots, WIDE),
+        bf(slots, 2 * HEAD_DIM),
+        bf(slots, 2 * HEAD_DIM),
         bf(slots, WIDE),
         bf(slots, WIDE),
         f32(own, HEADS, HEAD_DIM),
@@ -656,12 +743,17 @@
         bf(n, own, HEAD_DIM),
         bf(n, own, HEAD_DIM),
         f32(rows, HEAD_DIM),
-        bf(4, rows, HEAD_DIM),
-        bf(4, rows, HEAD_DIM),
+        bf(4, rows, 128),
+        bf(4, rows, 128),
         bf(2, 2, CHIPS, own, width),
         bf(2, CHIPS, own, width),
         bf(2, CHIPS, own, width),
         bf(2, CHIPS, own, width),
+        bf(16, 128),
+        bf(4, 16, 128),
+        bf(slots, 128),
+        bf(slots, 128),
+        f32(8, 128),
         dma((8,)),
         dma((2, CHIPS)),
         dma((2, CHIPS)),
@@ -684,10 +776,14 @@
         dma((2, CHIPS)),
         dma((2, CHIPS)),
         dma((2,)),
+        dma((4,)),
+        dma((4,)),
+        dma((planes,)),
+        dma((planes,)),
     ]
     return pl.pallas_call(
         functools.partial(layer_kernel, n, planes),
-        out_shape=jax.ShapeDtypeStruct((own, width), BF16),
+        out_shape=jax.ShapeDtypeStruct((own, width), F32),
         in_specs=[pl.BlockSpec(memory_space=pltpu.VMEM)] * len(small)
         + [pl.BlockSpec(memory_space=pl.ANY)] * len(large),
         out_specs=pl.BlockSpec(memory_space=pltpu.VMEM),
@@ -717,33 +813,19 @@
     req_group,
     tail_len,
 ):
-    me = lax.axis_index("tp")
-    own = hidden_in.shape[0]
-    rows = own * n
-    req_len = lookup(prompt_len, req_group)
-    position = req_len + tail_len
-    frequency = jnp.exp(jnp.arange(HALF).astype(F32) * (-math.log(10000.0) / HALF))
-    angles = position.astype(F32)[:, None] * frequency[None, :]
-    req_home = lookup(group_home, req_group)
-    req_start = lookup(group_starts(prompt_len, group_home), req_group)
-    order = jnp.arange(rows, dtype=jnp.int32)
-    before = (req_home[None, :] == req_home[:, None]) & (order[None, :] < order[:, None])
-    slot = req_home * SLOTS + jnp.sum(before.astype(jnp.int32), axis=1)
-    slot_ids = jnp.arange(planes * SLOTS, dtype=jnp.int32)
-    pick = (slot_ids[:, None] == slot[None, :]).astype(BF16)
-    pick_t = (slot_ids[None, :] == slot[:, None]).astype(BF16)
-    stop = req_start + req_len
-    bounds = jnp.stack([req_start // 64, req_start % 64, stop // 64, stop % 64], axis=1).astype(BF16)
-    bounds = jnp.pad(bounds, ((0, 0), (0, 124)))
-    own_len = lax.dynamic_slice_in_dim(tail_len, me * own, own, 0)
-    tail = tail_keys.shape[1]
-    seen = (jnp.arange(tail, dtype=jnp.int32)[None, :] < own_len[:, None]).astype(F32)
     return layer(
         n,
         planes,
-        (hidden_in, norm_gains, jnp.cos(angles), jnp.sin(angles), pick, pick_t, bounds, seen),
+        (
+            hidden_in,
+            norm_gains,
+            prompt_len[None],
+            group_home[None],
+            req_group[None],
+            tail_len[None],
+        ),
         (w_qkv, w_out, w_gate_up, w_down, prompt_keys, prompt_values, tail_keys, tail_values),
-    )
+    ).astype(BF16)
 
 
 def solution(mesh):

time: 105 us -> 91.8 us (0.87)
  Pallas kernels: 95.8 us -> 89.5 us
  other arithmetic: 5.53 us -> 1.44 us
  local copies, waits for them, and re-layouts: 2.84 us -> 0 us
    pallas_call x1, Pallas kernels: 95.8 us -> 89.5 us  [layer(): pl.pallas_call(functools.partial(layer_kernel, n, planes), out_shape=jax....]
    reduce_sum x3 -> x0, other arithmetic: 1.88 us -> none  [the longest x1 0.91 us: group_starts(): jnp.sum(jnp.where(same_home & earlier, prompt_len[None, :], 0), axis=1)]
    unnamed x1 -> x0, local copies, waits for them, and re-layouts: 1.37 us -> none
where the time goes in v3:
time: 91.8 us; the launch traced here: 90.9 us
  Pallas kernels  89.5 us (97%)
  other arithmetic  1.44 us (2%)
    pallas_call x1, Pallas kernels, layer(): pl.pallas_call(functools.partial(layer_kernel, n, planes), out_shape=jax....  89.5 us

profile of v3, /device:TPU:1, one launch (start us, length us, event | category | flops | bytes accessed | tf_op | source)
XLA Modules:
  0.0 90.9 jit_solution(3091469330005734145)
XLA Ops:
  0.0 89.5 %layer.1 = f32[4,3584]{1,0:T(4,128)} custom-call(bf16[4,3584]{1,0:T(4,128)(2,1)} %hidden_ref.1, f32[4,3584]{1,0:T(4,128)} %gains_ref.1, s32[1,80]{1,0:T(1,128)} %bitcast.4, s32[1,80]{1,0:T(1,128)} %bitcast.5, s32[1,128]{1,0:T(1,128)} %bitcast.6, s32[1,128]{1,0:T(1,128)} %bitcast.7, bf16[3584,256]{1,0:T(8,128)(2,1)} %w_qkv_hbm.1, ...), custom_call_target="tpu_custom_call" | custom-call | tf_op jit(solution)/shard_map/layer/pallas_call | solution.py:784
  89.5 1.4 %convert_element_type.3 = bf16[4,3584]{1,0:T(4,128)(2,1)} convert(f32[4,3584]{1,0:T(4,128)} %layer.1) | non-fusion elementwise | flops 14336 | bytes 86016 | tf_op jit(solution)/shard_map/convert_element_type | solution.py:828

commit v4 on v3

--- a/solution.py
+++ b/solution.py
@@ -20,7 +20,7 @@
 MESH = pl.DeviceIdType.MESH
 F32 = jnp.float32
 BF16 = jnp.bfloat16
-CHIP_STEPS = (1, 15, 2, 14, 3, 13, 4, 12, 5, 11, 6, 10, 7, 9, 8)
+CHIP_STEPS = (10, 6, 9, 14, 11, 5, 7, 13, 15, 2, 8, 1, 4, 3, 12)
 PLANE_STEPS = (4, 3, 5, 2, 6, 1, 7)
 
 
@@ -47,7 +47,16 @@
 
 
 def server_of(head, m):
-    return jnp.where(head < 4, (m * 4 + head) * 2, ((head - 4) * 4 + m) * 2 + 1)
+    column, line = column_of(head), row_of(head)
+    return jnp.where(lax.rem(head, 4) < 2, (m * 4 + column) * 2, (line * 4 + m) * 2 + 1)
+
+
+def column_of(head):
+    return 2 * (head % 4) + head // 4 if isinstance(head, int) else 2 * lax.rem(head, 4) + head // 4
+
+
+def row_of(head):
+    return 2 * (head // 4) + (head % 4 if isinstance(head, int) else lax.rem(head, 4)) - 2
 
 
 def layer_kernel(
@@ -139,7 +148,7 @@
     chip, core = me // 2, lax.rem(me, 2)
     x, y = chip // 4, lax.rem(chip, 4)
     partner = chip * 2 + 1 - core
-    served = jnp.where(core == 0, y, 4 + x)
+    served = jnp.where(core == 0, y // 2 + 4 * lax.rem(y, 2), 2 + lax.rem(x, 2) + 4 * (x // 2))
     quarter = jnp.where(core == 0, x, y)
     own, width = hidden_ref.shape
     rows = own * n
@@ -174,11 +183,17 @@
     slab_ref[0] = rms_scale(hidden_ref[...], gains_ref[0:1, :]).astype(BF16)
     pl.semaphore_wait(barrier, n - 1 + planes - 1)
 
+    def chip_at(step):
+        return lax.rem(x + step // 4, 4) * 4 + lax.rem(y + step % 4, 4)
+
+    def chip_from(step):
+        return lax.rem(x + 4 - step // 4, 4) * 4 + lax.rem(y + 4 - step % 4, 4)
+
     def at_chip(step):
-        return lax.rem(chip + step, CHIPS) * 2 + core
+        return chip_at(step) * 2 + core
 
     def from_chip(step):
-        return lax.rem(chip + CHIPS - step, CHIPS) * 2 + core
+        return chip_from(step) * 2 + core
 
     def gather_copy(turn, step):
         return remote(
@@ -223,60 +238,67 @@
         for step in (0, *CHIP_STEPS):
             forward_copy(turn, step).wait_send()
 
-    def half_copy(turn, step):
-        group = pl.ds(lax.rem(x + step, 4) * 4, 4)
-        return remote(
-            part_ref.at[turn, 1 - core, group],
-            half_ref.at[turn, group],
-            hf_send.at[turn, step],
-            hf_recv.at[turn, step],
+    middle = width // 2
+
+    def half_copy(turn, side):
+        span = slice(side * middle, (side + 1) * middle)
+        return remote(
+            part_ref.at[turn, 1 - core, :, :, span],
+            half_ref.at[turn, :, :, span],
+            hf_send.at[turn, side],
+            hf_recv.at[turn, side],
             "tp",
             partner,
         )
 
-    def scatter_copy(turn, step):
-        target = lax.rem(chip + step, CHIPS)
-        return remote(
-            chip_ref.at[turn, target],
-            got_ref.at[turn, chip],
-            rs_send.at[turn, step],
-            rs_recv.at[turn, step],
+    def scatter_copy(turn, side, step):
+        span = slice(side * middle, (side + 1) * middle)
+        return remote(
+            chip_ref.at[turn, chip_at(step), :, span],
+            got_ref.at[turn, chip, :, span],
+            rs_send.at[turn, side, step],
+            rs_recv.at[turn, side, step],
             "tp",
-            target * 2 + core,
+            at_chip(step),
         )
 
     def project(turn, left, weight_ref):
-        def chunk(j, carry):
-            columns = pl.ds(pl.multiple_of(j * 512, 512), 512)
-            block = jnp.dot(left, weight_ref[:, columns], preferred_element_type=F32)
-            for d in range(n):
-                part_ref[turn, d % 2, d // 2, :, columns] = block[own * d : own * d + own, :].astype(BF16)
-            return carry
-
-        lax.fori_loop(0, width // 512, chunk, 0)
+        piece = middle // 2
+        for side in range(2):
+
+            def chunk(j, carry):
+                columns = pl.ds(pl.multiple_of((2 * side + j) * piece, 128), piece)
+                block = jnp.dot(left, weight_ref[:, columns], preferred_element_type=F32)
+                for d in range(n):
+                    part_ref[turn, d % 2, d // 2, :, columns] = block[own * d : own * d + own, :].astype(BF16)
+                return carry
+
+            lax.fori_loop(0, 2, chunk, 0)
+            half_copy(turn, side).start()
 
     def reduce_scatter(turn):
-        for step in (0, 1, 2, 3):
-            half_copy(turn, step).start()
-        for step in (0, 1, 2, 3):
-            half_copy(turn, step).wait_recv()
-        for step in (0, *CHIP_STEPS):
-            target = lax.rem(chip + step, CHIPS)
-            both = part_ref[turn, core, target].astype(F32) + half_ref[turn, target].astype(F32)
-            chip_ref[turn, target] = both.astype(BF16)
-            if step:
-                scatter_copy(turn, step).start()
+        for side in range(2):
+            span = slice(side * middle, (side + 1) * middle)
+            half_copy(turn, side).wait_recv()
+            for step in (*CHIP_STEPS, 0):
+                target = chip_at(step)
+                both = part_ref[turn, core, target, :, span].astype(F32)
+                both = both + half_ref[turn, target, :, span].astype(F32)
+                chip_ref[turn, target, :, span] = both.astype(BF16)
+                if step:
+                    scatter_copy(turn, side, step).start()
         total = chip_ref[turn, chip].astype(F32)
         for step in CHIP_STEPS:
-            scatter_copy(turn, step).wait_recv()
-            total = total + got_ref[turn, lax.rem(chip + CHIPS - step, CHIPS)].astype(F32)
+            scatter_copy(turn, 0, step).wait_recv()
+            scatter_copy(turn, 1, step).wait_recv()
+            total = total + got_ref[turn, chip_from(step)].astype(F32)
         return total
 
     def scatter_drain(turn):
-        for step in (0, 1, 2, 3):
-            half_copy(turn, step).wait_send()
-        for step in CHIP_STEPS:
-            scatter_copy(turn, step).wait_send()
+        for side in range(2):
+            half_copy(turn, side).wait_send()
+            for step in CHIP_STEPS:
+                scatter_copy(turn, side, step).wait_send()
 
     gather_start(0)
 
@@ -349,7 +371,9 @@
     cosine, sine = jnp.cos(angles), jnp.sin(angles)
 
     def kv_server(head):
-        return jnp.where(head < 4, (x * 4 + head) * 2, ((head - 4) * 4 + y) * 2 + 1)
+        if head % 4 < 2:
+            return (x * 4 + column_of(head)) * 2
+        return (row_of(head) * 4 + y) * 2 + 1
 
     def kv_source(slot):
         mate = lax.rem(slot, 2)
@@ -359,7 +383,7 @@
     piece = keys_ref.shape[0]
 
     def kv_copy(i, head):
-        slot = (y if head < 4 else x) * 2 + core
+        slot = (y if head % 4 < 2 else x) * 2 + core
         return remote(
             pieces[i][0].at[:, head * HEAD_DIM : (head + 1) * HEAD_DIM],
             pieces[i][1].at[pl.ds(slot * piece, piece)],
@@ -370,7 +394,7 @@
         )
 
     def kv_local(i, head):
-        slot = (y if head < 4 else x) * 2 + core
+        slot = (y if head % 4 < 2 else x) * 2 + core
         return pltpu.make_async_copy(
             pieces[i][0].at[:, head * HEAD_DIM : (head + 1) * HEAD_DIM],
             pieces[i][1].at[pl.ds(slot * piece, piece)],
@@ -430,6 +454,18 @@
     own_heads[me] = head_slabs[me]
 
     for i in range(2):
+        loads[i].wait()
+        for head in range(KV_HEADS):
+
+            @pl.when(kv_server(head) != me)
+            def _():
+                kv_copy(i, head).start()
+
+            @pl.when(kv_server(head) == me)
+            def _():
+                kv_local(i, head).start()
+
+    for i in range(2):
 
         @pl.when(2 * served + i == me)
         def _():
@@ -460,18 +496,6 @@
     for step in PLANE_STEPS:
         z_copy(0, step).start()
     guest_ref[here, :] = visit_ref[here, :]
-
-    for i in range(2):
-        loads[i].wait()
-        for head in range(KV_HEADS):
-
-            @pl.when(kv_server(head) != me)
-            def _():
-                kv_copy(i, head).start()
-
-            @pl.when(kv_server(head) == me)
-            def _():
-                kv_local(i, head).start()
 
     for step in range(1, n):
         owner_copy(step).wait_recv()
@@ -771,10 +795,10 @@
         dma((n,)),
         dma((4,)),
         dma((4,)),
-        dma((2, 4)),
-        dma((2, 4)),
-        dma((2, CHIPS)),
-        dma((2, CHIPS)),
+        dma((2, 2)),
+        dma((2, 2)),
+        dma((2, 2, CHIPS)),
+        dma((2, 2, CHIPS)),
         dma((2,)),
         dma((4,)),
         dma((4,)),

time: 91.8 us -> 86.2 us (0.939)
  Pallas kernels: 89.5 us -> 84.5 us
    pallas_call x1, Pallas kernels: 89.5 us -> 84.5 us  [layer(): pl.pallas_call(functools.partial(layer_kernel, n, planes), out_shape=jax....]
where the time goes in v4:
time: 86.2 us; the launch traced here: 86 us
  Pallas kernels  84.5 us (98%)
  other arithmetic  1.44 us (2%)
    pallas_call x1, Pallas kernels, layer(): pl.pallas_call(functools.partial(layer_kernel, n, planes), out_shape=jax....  84.5 us

profile of v4, /device:TPU:1, one launch (start us, length us, event | category | flops | bytes accessed | tf_op | source)
XLA Modules:
  0.0 86.0 jit_solution(10057492428914014336)
XLA Ops:
  0.0 84.5 %layer.1 = f32[4,3584]{1,0:T(4,128)} custom-call(bf16[4,3584]{1,0:T(4,128)(2,1)} %hidden_ref.1, f32[4,3584]{1,0:T(4,128)} %gains_ref.1, s32[1,80]{1,0:T(1,128)} %bitcast.4, s32[1,80]{1,0:T(1,128)} %bitcast.5, s32[1,128]{1,0:T(1,128)} %bitcast.6, s32[1,128]{1,0:T(1,128)} %bitcast.7, bf16[3584,256]{1,0:T(8,128)(2,1)} %w_qkv_hbm.1, ...), custom_call_target="tpu_custom_call" | custom-call | tf_op jit(solution)/shard_map/layer/pallas_call | solution.py:808
  84.5 1.4 %convert_element_type.3 = bf16[4,3584]{1,0:T(4,128)(2,1)} convert(f32[4,3584]{1,0:T(4,128)} %layer.1) | non-fusion elementwise | flops 14336 | bytes 86016 | tf_op jit(solution)/shard_map/convert_element_type | solution.py:852

commit v5 on v4

--- a/solution.py
+++ b/solution.py
@@ -20,7 +20,7 @@
 MESH = pl.DeviceIdType.MESH
 F32 = jnp.float32
 BF16 = jnp.bfloat16
-CHIP_STEPS = (10, 6, 9, 14, 11, 5, 7, 13, 15, 2, 8, 1, 4, 3, 12)
+DIRECT_STEPS = (14, 13, 15, 12, 6, 5, 7, 4, 2, 1, 3)
 PLANE_STEPS = (4, 3, 5, 2, 6, 1, 7)
 
 
@@ -111,6 +111,7 @@
     half_ref,
     chip_ref,
     got_ref,
+    relay_ref,
     word_ref,
     words_ref,
     bound_ref,
@@ -183,11 +184,18 @@
     slab_ref[0] = rms_scale(hidden_ref[...], gains_ref[0:1, :]).astype(BF16)
     pl.semaphore_wait(barrier, n - 1 + planes - 1)
 
+    a, b = jnp.where(core == 0, x, y), jnp.where(core == 0, y, x)
+
+    def chip_of(i, j):
+        return jnp.where(core == 0, i * 4 + j, j * 4 + i)
+
     def chip_at(step):
-        return lax.rem(x + step // 4, 4) * 4 + lax.rem(y + step % 4, 4)
+        return chip_of(lax.rem(a + step // 4, 4), lax.rem(b + step % 4, 4))
 
     def chip_from(step):
-        return lax.rem(x + 4 - step // 4, 4) * 4 + lax.rem(y + 4 - step % 4, 4)
+        return chip_of(lax.rem(a + 4 - step // 4, 4), lax.rem(b + 4 - step % 4, 4))
+
+    neighbour = chip_of(lax.rem(a + 3, 4), b) * 2 + core
 
     def at_chip(step):
         return chip_at(step) * 2 + core
@@ -216,26 +224,44 @@
             partner,
         )
 
+    def relay_copy(turn, j):
+        source = from_chip(12 + j)
+        return remote(
+            slabs_ref.at[turn, source],
+            slabs_ref.at[turn, source],
+            ag_send.at[turn, 8 + j],
+            ag_recv.at[turn, 8 + j],
+            "tp",
+            neighbour,
+        )
+
     def gather_start(turn):
-        for step in CHIP_STEPS:
+        for step in DIRECT_STEPS:
             gather_copy(turn, step).start()
         forward_copy(turn, 0).start()
         slabs_ref[turn, me] = slab_ref[turn]
 
     def gather_finish(turn):
-        for step in CHIP_STEPS:
+        for step in DIRECT_STEPS:
             gather_copy(turn, step).wait_recv()
+            if step >= 12:
+                relay_copy(turn, step - 12).start()
             forward_copy(turn, step).start()
-        for step in (0, *CHIP_STEPS):
+        for j in (2, 1, 3, 0):
+            gather_copy(turn, 8 + j).wait_recv()
+            forward_copy(turn, 8 + j).start()
+        for step in range(CHIPS):
             forward_copy(turn, step).wait_recv()
         for group in range(rows // 16):
             four = [slabs_ref[turn, group * 4 + i].astype(F32) for i in range(4)]
             rows_ref[group * 16 : group * 16 + 16, :] = jnp.concatenate(four, axis=0).astype(BF16)
 
     def gather_drain(turn):
-        for step in CHIP_STEPS:
+        for step in DIRECT_STEPS:
             gather_copy(turn, step).wait_send()
-        for step in (0, *CHIP_STEPS):
+        for j in range(4):
+            relay_copy(turn, j).wait_send()
+        for step in range(CHIPS):
             forward_copy(turn, step).wait_send()
 
     middle = width // 2
@@ -276,19 +302,46 @@
             lax.fori_loop(0, 2, chunk, 0)
             half_copy(turn, side).start()
 
+    def lift_copy(turn, side, j):
+        span = slice(side * middle, (side + 1) * middle)
+        return remote(
+            chip_ref.at[turn, chip_at(8 + j), :, span],
+            relay_ref.at[turn, j, :, span],
+            rs_send.at[turn, side, 8 + j],
+            rs_recv.at[turn, side, 8 + j],
+            "tp",
+            neighbour,
+        )
+
     def reduce_scatter(turn):
         for side in range(2):
             span = slice(side * middle, (side + 1) * middle)
             half_copy(turn, side).wait_recv()
-            for step in (*CHIP_STEPS, 0):
+
+            def both(step):
                 target = chip_at(step)
-                both = part_ref[turn, core, target, :, span].astype(F32)
-                both = both + half_ref[turn, target, :, span].astype(F32)
-                chip_ref[turn, target, :, span] = both.astype(BF16)
-                if step:
+                total = part_ref[turn, core, target, :, span].astype(F32)
+                return target, total + half_ref[turn, target, :, span].astype(F32)
+
+            for step in (10, 9, 11, 8, 6, 5, 7, 4, 2, 1, 3, 0):
+                target, total = both(step)
+                chip_ref[turn, target, :, span] = total.astype(BF16)
+                if step >= 8:
+                    lift_copy(turn, side, step - 8).start()
+                elif step:
                     scatter_copy(turn, side, step).start()
+        for side in range(2):
+            span = slice(side * middle, (side + 1) * middle)
+            for j in (2, 1, 3, 0):
+                lift_copy(turn, side, j).wait_recv()
+                target = chip_at(12 + j)
+                total = part_ref[turn, core, target, :, span].astype(F32)
+                total = total + half_ref[turn, target, :, span].astype(F32)
+                total = total + relay_ref[turn, j, :, span].astype(F32)
+                chip_ref[turn, target, :, span] = total.astype(BF16)
+                scatter_copy(turn, side, 12 + j).start()
         total = chip_ref[turn, chip].astype(F32)
-        for step in CHIP_STEPS:
+        for step in (6, 5, 7, 4, 2, 1, 3, 14, 13, 15, 12):
             scatter_copy(turn, 0, step).wait_recv()
             scatter_copy(turn, 1, step).wait_recv()
             total = total + got_ref[turn, chip_from(step)].astype(F32)
@@ -297,8 +350,10 @@
     def scatter_drain(turn):
         for side in range(2):
             half_copy(turn, side).wait_send()
-            for step in CHIP_STEPS:
+            for step in DIRECT_STEPS:
                 scatter_copy(turn, side, step).wait_send()
+            for j in range(4):
+                lift_copy(turn, side, j).wait_send()
 
     gather_start(0)
 
@@ -773,6 +828,7 @@
         bf(2, CHIPS, own, width),
         bf(2, CHIPS, own, width),
         bf(2, CHIPS, own, width),
+        bf(2, 4, own, width),
         bf(16, 128),
         bf(4, 16, 128),
         bf(slots, 128),

time: 86.2 us -> 88.8 us (1.030)
  Pallas kernels: 84.5 us -> 86.4 us
    pallas_call x1, Pallas kernels: 84.5 us -> 86.4 us  [layer(): pl.pallas_call(functools.partial(layer_kernel, n, planes), out_shape=jax....]
where the time goes in v5:
time: 88.8 us; the launch traced here: 87.9 us
  Pallas kernels  86.4 us (97%)
  other arithmetic  1.44 us (2%)
    pallas_call x1, Pallas kernels, layer(): pl.pallas_call(functools.partial(layer_kernel, n, planes), out_shape=jax....  86.4 us

profile of v5, /device:TPU:1, one launch (start us, length us, event | category | flops | bytes accessed | tf_op | source)
XLA Modules:
  0.0 87.9 jit_solution(3464170609363378943)
XLA Ops:
  0.0 86.4 %layer.1 = f32[4,3584]{1,0:T(4,128)} custom-call(bf16[4,3584]{1,0:T(4,128)(2,1)} %hidden_ref.1, f32[4,3584]{1,0:T(4,128)} %gains_ref.1, s32[1,80]{1,0:T(1,128)} %bitcast.4, s32[1,80]{1,0:T(1,128)} %bitcast.5, s32[1,128]{1,0:T(1,128)} %bitcast.6, s32[1,128]{1,0:T(1,128)} %bitcast.7, bf16[3584,256]{1,0:T(8,128)(2,1)} %w_qkv_hbm.1, ...), custom_call_target="tpu_custom_call" | custom-call | tf_op jit(solution)/shard_map/layer/pallas_call | solution.py:864
  86.5 1.4 %convert_element_type.3 = bf16[4,3584]{1,0:T(4,128)(2,1)} convert(f32[4,3584]{1,0:T(4,128)} %layer.1) | non-fusion elementwise | flops 14336 | bytes 86016 | tf_op jit(solution)/shard_map/convert_element_type | solution.py:908

commit v6 on v4

--- a/solution.py
+++ b/solution.py
@@ -16,7 +16,6 @@
 CHIPS = 16
 NORM_EPS = 1e-06
 SOFT_CAP = 50.0
-WIDE = 2 * HEAD_DIM + 128
 MESH = pl.DeviceIdType.MESH
 F32 = jnp.float32
 BF16 = jnp.bfloat16
@@ -116,6 +115,9 @@
     bound_ref,
     limit_ref,
     table_ref,
+    reply_words,
+    answer_words,
+    select_ref,
     load_sem,
     ag_send,
     ag_recv,
@@ -142,6 +144,8 @@
     wd_recv,
     lm_send,
     lm_recv,
+    bw_send,
+    bw_recv,
 ):
     me = lax.axis_index("tp")
     plane = lax.axis_index("grp")
@@ -349,6 +353,11 @@
     bounds = jnp.zeros((rows, 128), F32)
     for i, value in enumerate((req[:, 3:4], req[:, 4:5], *split(req_stop))):
         bounds = jnp.where(along == i, value, bounds)
+    at = lax.broadcasted_iota(jnp.int32, (1, planes * 128), 1)
+    of_home = req[:, 2:3] == (at // 128).astype(F32)
+    shift = (lax.rem(plane, planes // 2) * SLOTS).astype(F32)
+    of_slot = rank + shift == lax.rem(at, 128).astype(F32)
+    select_ref[...] = (of_home & of_slot).astype(BF16)
     bound_ref[...] = jnp.dot(pick, bounds.astype(BF16), preferred_element_type=F32).astype(BF16)
 
     def limit_copy(step):
@@ -580,6 +589,18 @@
     device = jnp.where(core == 0, (x * 4 + pair_of) * 2 + mate, (pair_of * 4 + y) * 2 + mate)
     spot = (device * piece + lax.rem(at, piece)).astype(F32)
     many = planes * SLOTS // 2
+
+    def back_copy(step):
+        peer = lax.rem(plane + step, planes)
+        return remote(
+            reply_words.at[peer // (planes // 2)],
+            answer_words.at[plane],
+            bw_send.at[step],
+            bw_recv.at[step],
+            "grp",
+            peer,
+        )
+
     lanes = lax.broadcasted_iota(jnp.int32, (many, 128), 1)
     for j in range(2):
         part = slice(j * many, (j + 1) * many)
@@ -603,17 +624,28 @@
             high = den.astype(BF16).astype(F32)
             words = jnp.where(lanes == 2 * i, high, words)
             words = jnp.where(lanes == 2 * i + 1, den - high, words)
-        reply_ref[part, 2 * HEAD_DIM :] = words.astype(BF16)
-    for step in PLANE_STEPS:
-        z_copy(1, step).start()
+        reply_words[j] = turned(unit[:16, :], words.astype(BF16))[:4, :].astype(BF16)
+        for i in range(planes // 2):
+            guest = j * (planes // 2) + i
+            away = lax.rem(guest + planes - plane, planes)
+
+            @pl.when(guest != plane)
+            def _():
+                z_copy(1, away).start()
+                back_copy(away).start()
+
     answer_ref[here, :] = reply_ref[here, :]
+    answer_words[plane] = reply_words[plane // (planes // 2)]
     for step in PLANE_STEPS:
         z_copy(1, step).wait_recv()
+        back_copy(step).wait_recv()
 
     back = jnp.dot(pick_t, answer_ref[...], preferred_element_type=F32).astype(BF16)
     for i in range(4):
         parts_ref[i] = back[:, i * 128 : (i + 1) * 128]
-    word_ref[...] = turned(unit[:16, :], back[:, 2 * HEAD_DIM :]).astype(BF16)
+    lines = jnp.concatenate([answer_words[p].astype(F32) for p in range(planes)], axis=1)
+    lines = jnp.concatenate([lines, jnp.zeros((12, lines.shape[1]), F32)], axis=0).astype(BF16)
+    word_ref[...] = turned(lines, select_ref[...]).astype(BF16)
 
     def join_copy(i):
         return remote(
@@ -709,6 +741,7 @@
             z_copy(turn, step).wait_send()
     for step in PLANE_STEPS:
         limit_copy(step).wait_send()
+        back_copy(step).wait_send()
     for i in range(2):
         for head in range(KV_HEADS):
 
@@ -758,8 +791,8 @@
         bf(2, rows, HEAD_DIM),
         bf(slots, 2 * HEAD_DIM),
         bf(slots, 2 * HEAD_DIM),
-        bf(slots, WIDE),
-        bf(slots, WIDE),
+        bf(slots, 2 * HEAD_DIM),
+        bf(slots, 2 * HEAD_DIM),
         f32(own, HEADS, HEAD_DIM),
         f32(own, HEADS, HEAD_DIM),
         f32(own, HEADS, HEAD_DIM),
@@ -778,6 +811,9 @@
         bf(slots, 128),
         bf(slots, 128),
         f32(8, 128),
+        bf(2, 4, 128),
+        bf(planes, 4, 128),
+        bf(rows, planes * 128),
         dma((8,)),
         dma((2, CHIPS)),
         dma((2, CHIPS)),
@@ -802,6 +838,8 @@
         dma((2,)),
         dma((4,)),
         dma((4,)),
+        dma((planes,)),
+        dma((planes,)),
         dma((planes,)),
         dma((planes,)),
     ]

time: 86.2 us -> 84.2 us (0.977)
  the two profiles are of different devices: /device:TPU:1 before, /device:TPU:64 now
where the time goes in v6:
time: 84.2 us; the launch traced here: 84 us
  Pallas kernels  82.6 us (98%)
  other arithmetic  1.44 us (2%)
    pallas_call x1, Pallas kernels, layer(): pl.pallas_call(functools.partial(layer_kernel, n, planes), out_shape=jax....  82.6 us

profile of v6, /device:TPU:64, one launch (start us, length us, event | category | flops | bytes accessed | tf_op | source)
XLA Modules:
  0.0 84.0 jit_solution(523102288847813976)
XLA Ops:
  0.0 82.6 %layer.1 = f32[4,3584]{1,0:T(4,128)} custom-call(bf16[4,3584]{1,0:T(4,128)(2,1)} %hidden_ref.1, f32[4,3584]{1,0:T(4,128)} %gains_ref.1, s32[1,80]{1,0:T(1,128)} %bitcast.4, s32[1,80]{1,0:T(1,128)} %bitcast.5, s32[1,128]{1,0:T(1,128)} %bitcast.6, s32[1,128]{1,0:T(1,128)} %bitcast.7, bf16[3584,256]{1,0:T(8,128)(2,1)} %w_qkv_hbm.1, ...), custom_call_target="tpu_custom_call" | custom-call | tf_op jit(solution)/shard_map/layer/pallas_call | solution.py:846
  82.6 1.4 %convert_element_type.3 = bf16[4,3584]{1,0:T(4,128)(2,1)} convert(f32[4,3584]{1,0:T(4,128)} %layer.1) | non-fusion elementwise | flops 14336 | bytes 86016 | tf_op jit(solution)/shard_map/convert_element_type | solution.py:890

commit v7 on v6

--- a/solution.py
+++ b/solution.py
@@ -443,7 +443,9 @@
             server_of(chip, m),
         )
 
-    for m in range(4):
+    base = jnp.where(lax.rem(chip, 4) < 2, x, y)
+    for away in (2, 1, 3, 0):
+        m = lax.rem(base + away, 4)
 
         @pl.when((me < HEADS) & (server_of(chip, m) != me))
         def _():

time: 84.2 us -> 83.6 us (level)
  no operation moved by 1% of the time
where the time goes in v7:
time: 83.6 us; the launch traced here: 83.4 us
  Pallas kernels  82 us (98%)
  other arithmetic  1.44 us (2%)
    pallas_call x1, Pallas kernels, layer(): pl.pallas_call(functools.partial(layer_kernel, n, planes), out_shape=jax....  82 us

profile of v7, /device:TPU:64, one launch (start us, length us, event | category | flops | bytes accessed | tf_op | source)
XLA Modules:
  0.0 83.4 jit_solution(7561649933415385507)
XLA Ops:
  0.0 82.0 %layer.1 = f32[4,3584]{1,0:T(4,128)} custom-call(bf16[4,3584]{1,0:T(4,128)(2,1)} %hidden_ref.1, f32[4,3584]{1,0:T(4,128)} %gains_ref.1, s32[1,80]{1,0:T(1,128)} %bitcast.4, s32[1,80]{1,0:T(1,128)} %bitcast.5, s32[1,128]{1,0:T(1,128)} %bitcast.6, s32[1,128]{1,0:T(1,128)} %bitcast.7, bf16[3584,256]{1,0:T(8,128)(2,1)} %w_qkv_hbm.1, ...), custom_call_target="tpu_custom_call" | custom-call | tf_op jit(solution)/shard_map/layer/pallas_call | solution.py:848
  82.0 1.4 %convert_element_type.3 = bf16[4,3584]{1,0:T(4,128)(2,1)} convert(f32[4,3584]{1,0:T(4,128)} %layer.1) | non-fusion elementwise | flops 14336 | bytes 86016 | tf_op jit(solution)/shard_map/convert_element_type | solution.py:892
